TPU v7x, 256 devices: a whole 4x4x8 slice. The times are simulated.
256 devices in a mesh: rep: 32 (over y, z_hi, core), dom: 8 (over z_lo, x).
Axes of the slice: x: 4, y: 4, z: 8 (z_hi: 4, z_lo: 2; z = z_hi * 2 + z_lo), core: 2. Of those that a mesh axis runs over, the one named last changes fastest.
Arguments:
- atomic_locations: float32 [3, 32, 65536], P(None, 'rep', 'dom'), may hold values from -9 to 9
- atomic_speeds: float32 [3, 32, 65536], P(None, 'rep', 'dom'), may hold values from -6 to 6
- atomic_properties: float32 [3, 65536], P(None, 'dom'), as said below
- resident_tile_members: int32 [2, 32, 512], P(None, 'rep', 'dom'), may hold values from 0 to 63
- resident_tile_tally: int32 [32, 8], P('rep', 'dom'), may hold values from 1 to 64, as said below
- top_edge_groups: int32 [32, 256], P('rep', 'dom'), may hold values from 0 to 63, as said below
- bottom_edge_groups: int32 [32, 256], P('rep', 'dom'), may hold values from 0 to 63, as said below
- boundary_tile_slots: int32 [2, 32, 256], P(None, 'rep', 'dom'), may hold values from 0 to 31
- boundary_tile_tally: int32 [32, 8], P('rep', 'dom'), may hold values from 1 to 32, as said below
- spring_links: int32 [2, 32768], P(None, 'dom'), may hold values from 0 to 8191
- thermal_levels: float32 [32], replicated, may hold values from 1 to 4
- exchange_mate: int32 [32], replicated, may hold values from 0 to 31, as said below
Outputs:
- positions_out: float32 [3, 32, 65536], P(None, 'rep', 'dom')
- velocities_out: float32 [3, 32, 65536], P(None, 'rep', 'dom')
Inputs may be any that keep to these rules, and one draw needn't show every extreme that they name: `resident_tile_tally`: the slots of one domain beyond its live count are padding. `boundary_tile_tally`: the slots of one domain beyond its live count are padding. `top_edge_groups`: the 32 entries of one domain are distinct clusters of that domain. `bottom_edge_groups`: the 32 entries of one domain are distinct clusters of that domain. exchange_mate[r] is r, r - 1 or r + 1, and exchange_mate[exchange_mate[r]] = r; the slot pairs 0, 1 and 30, 31 always swap. `atomic_properties`: row 0 charges, row 1 strengths between 0.5 and 1.5, row 2 inverse masses between 0.5 and 2.
All inputs are finite; a program needn't handle non-finite values.
Results may differ from a plain program's by a relative error of at most 0.0003.
Values sent between devices are 32-bit elements; how exact they have to be, the bound alone decides.
No kernel may reach another device: no remote copies, remote signals or barrier semaphores. Data moves between devices by JAX's collectives and lax.ppermute only.
A program may use at most 64 MiB of HBM per device.

v0:
```python
import functools
import math

import jax
import jax.numpy as jnp
from jax import lax
from jax.experimental import pallas as pl
from jax.experimental.pallas import tpu as pltpu
from jax.sharding import PartitionSpec as P

CA = 128
STEPS = 2
TIME_STEP = 0.05

F32 = jnp.float32
BF16 = jnp.bfloat16
LOG2E = 1.4426950408889634
ROWS = 8
ROUNDS = 4
PIECES = 4
LAG_SCALE = 3
LAG_SUM = 6
EDGE_SCALE = 3
EDGE_SUM = 6
BOND_PULL = 2
BOND_SPREAD = 4
VMEM_LIMIT = 20 << 20

SMEM = pl.BlockSpec(memory_space=pltpu.SMEM)
VMEM = pl.BlockSpec(memory_space=pltpu.VMEM)


def shifted(shard, axis, by):
    devices = lax.axis_size(axis)
    return lax.ppermute(shard, axis, [(i, (i + by) % devices) for i in range(devices)])


def swapped(shard, axis, start):
    devices = lax.axis_size(axis)
    pairs = []
    for i in range(start, devices - 1, 2):
        pairs += [(i, i + 1), (i + 1, i)]
    return lax.ppermute(shard, axis, pairs)


def halves(a):
    high = a.astype(BF16).astype(F32)
    return high, (a - high).astype(BF16).astype(F32)


def tile(cluster):
    return pl.ds(pl.multiple_of(cluster * ROWS, ROWS), ROWS)


def stack_rows(stack, base, rows):
    for k, row in enumerate(rows):
        count = rows[0].shape[0]
        if not hasattr(row, "shape"):
            row = jnp.full((count, CA), row, F32)
        stack[pl.ds(base * ROWS + k, count, stride=ROWS), :] = row


def position_parts(x, y, z):
    (xh, xm), (yh, ym), (zh, zm) = halves(x), halves(y), halves(z)
    x, y, z = xh + xm, yh + ym, zh + zm
    norm = x * x + y * y + z * z + 0.25
    nh, nm = halves(norm)
    return (xh, yh, zh), (xm, ym, zm), (nh, nm, norm - nh - nm)


def near_stack(stacks, base, high, middle, norm):
    stack_rows(stacks.at[0], base, [*high, norm[0], 1.0, 1.0, norm[2], 0.0])
    stack_rows(stacks.at[1], base, [*middle, norm[1], 0.0, 0.0, 0.0, 0.0])


def far_stack(stacks, high, middle, norm):
    twice = [-2.0 * a for a in high]
    stack_rows(stacks.at[2], 0, [*twice, 1.0, norm[0], norm[2], 1.0, 0.0])
    stack_rows(stacks.at[3], 0, [*[-2.0 * a for a in middle], 0.0, norm[1], 0.0, 0.0, 0.0])


def fill_ratio(ratio, rho, base):
    for c in range(rho.shape[0]):
        ratio[base + c] = jnp.transpose(jnp.broadcast_to(rho[c : c + 1], (CA, CA)))


def moment_stack(stack, base, x, y, z, strength):
    g = strength * math.exp(0.25)
    parts = [halves(a) for a in (g * x, g * y, g * z, g)]
    stack_rows(stack, base, [p[0] for p in parts] + [p[1] for p in parts])


def both_orders(stacks, k, c):
    h, m = stacks[k, tile(c), :], stacks[k + 1, tile(c), :]
    return (
        jnp.concatenate([h, m], axis=0).astype(BF16),
        jnp.concatenate([m, h], axis=0).astype(BF16),
    )


def fill_near(near, stacks, c):
    near[c] = both_orders(stacks, 0, c)[0]


def fill_far(far, stacks, c):
    far[c, 0], far[c, 1] = both_orders(stacks, 2, c)


def fill_moments(moments, stack, c):
    w = stack[tile(c), :]
    moments[c] = jnp.concatenate([w, jnp.zeros_like(w)], axis=0).astype(BF16)


def distances(near, far, pair, other):
    left = [near[i] for i, _ in (pair, other)]
    left = jnp.transpose(jnp.concatenate([left[0], left[0], left[1], left[1]], axis=0))
    right = [jnp.concatenate([far[j, 0], far[j, 1]], axis=0) for _, j in (pair, other)]
    zero = jnp.zeros_like(right[0])
    right = jnp.concatenate(
        [
            jnp.concatenate([right[0], zero], axis=1),
            jnp.concatenate([zero, right[1]], axis=1),
        ],
        axis=0,
    )
    both = jnp.dot(left, right, preferred_element_type=F32)
    return both[:, :CA], both[:, CA:]


def charge_ratio(charge, strength):
    return charge / strength * math.exp(-0.125)


def pair_scale(t, near_rho, far_rho):
    r = lax.rsqrt(t)
    c = jnp.exp2(t * (-0.5 * LOG2E)) + (near_rho * far_rho) * (r * r * r)
    high = c.astype(BF16)
    return high, (c - high.astype(F32)).astype(BF16)


def moment_sums(weights, scales):
    sums = jnp.dot(weights, scales, preferred_element_type=F32)[:ROWS]
    return sums[:, :CA] + sums[:, CA:]


def split(a, parts):
    return halves(a) if parts == 2 else (a,)


def bond_table(x, parts):
    half = x.shape[1] // 2

    def lay(v):
        flat = (3 * half, CA)
        return jnp.concatenate([v[:, :half].reshape(flat), v[:, half:].reshape(flat)], axis=1)

    return jnp.concatenate([lay(part) for part in split(x, parts)], axis=0).astype(BF16)


def bond_picks(picks, masks, atoms, start):
    size = atoms.shape[1]
    half = masks.shape[1]
    lane_id = lax.broadcasted_iota(jnp.int32, (2 * CA, size), 0).astype(F32).astype(BF16)
    row_id = lax.broadcasted_iota(jnp.int32, (half, size), 0)
    one, none = jnp.ones((), BF16), jnp.zeros((), BF16)
    for e in range(2):
        atom = atoms[e : e + 1]
        cluster = atom // CA
        lane = (atom % CA + cluster // half * CA).astype(F32).astype(BF16)
        hit = lane_id == jnp.broadcast_to(lane, lane_id.shape)
        picks[e, :, pl.ds(start, size)] = jnp.where(hit, one, none)
        mask = jnp.where(row_id == cluster % half, 1.0, 0.0)
        masks[e, :, pl.ds(start, size)] = mask.astype(BF16)


def bond_gather(table, picks, start, size):
    return [
        jnp.dot(table, picks[e, :, pl.ds(start, size)], preferred_element_type=F32)
        for e in range(2)
    ]


def bond_pull(rows, masks, start, size):
    half = masks.shape[1]
    parts = rows[0].shape[0] // (3 * half)
    ends = []
    for e in range(2):
        mask = masks[e, :, pl.ds(start, size)].astype(F32)
        both = sum(rows[e][k * 3 * half : (k + 1) * 3 * half] for k in range(parts))
        ends.append(jnp.sum(both.reshape(3, half, size) * mask[None], axis=1))
    return split(ends[1] - ends[0], parts)


def bond_scatter(pull, picks, masks, start, size):
    half = masks.shape[1]
    total = None
    for e, sign in enumerate((1.0, -1.0)):
        mask = masks[e, :, pl.ds(start, size)]
        spread = [
            mask * jnp.broadcast_to(sign * part[c : c + 1], (half, size)).astype(BF16)
            for part in pull
            for c in range(3)
        ]
        term = lax.dot_general(
            jnp.concatenate(spread, axis=0),
            picks[e, :, pl.ds(start, size)],
            (((1,), (1,)), ((), ())),
            preferred_element_type=F32,
        )
        total = term if total is None else total + term
    return total


def pair_moments(moments, i, j, scale):
    high, low = scale
    on_far = moment_sums(moments[i], jnp.concatenate([high, low], axis=1))
    turned = jnp.concatenate([jnp.transpose(high), jnp.transpose(low)], axis=1)
    return moment_sums(moments[j], turned), on_far


def local_kernel(first, pairs, tally, x_ref, props, *rest):
    if first:
        bonds, acc, bonded, picks, masks, ratio, *scratch = rest
    else:
        x_before, bonded_before, picks, masks, ratio, acc, bonded, *scratch = rest
    stacks, moment_rows, near, far, moments, rho, table, bond_sums = scratch
    clusters = x_ref.shape[1]
    half = clusters // 2
    group = pairs.shape[1] // ROUNDS
    size = picks.shape[2] // ROUNDS
    x, y, z = x_ref[0], x_ref[1], x_ref[2]
    parts = position_parts(x, y, z)
    rho[...] = charge_ratio(props[0], props[1])
    if first:
        fill_ratio(ratio, rho[...], 0)
    near_stack(stacks, 0, *parts)
    far_stack(stacks, *parts)
    moment_stack(moment_rows, 0, x, y, z, props[1])
    for c in range(clusters):
        fill_near(near, stacks, c)
        fill_far(far, stacks, c)
        fill_moments(moments, moment_rows, c)
    acc[...] = jnp.zeros_like(acc)
    if first:
        table[...] = bond_table(x_ref[...], 2)
    else:
        table[...] = bond_table(x_ref[...] - x_before[...], 1)
    bond_sums[...] = jnp.zeros_like(bond_sums)
    live = tally[0, 0]

    def round_of(block, carry):
        start = pl.multiple_of(block * size, size)
        if first:
            bond_picks(picks, masks, bonds[:, pl.ds(start, size)], start)
        slots = [block * group + k for k in range(group)]
        ends = [(pairs[0, s], pairs[1, s]) for s in slots]
        piece = size // PIECES
        steps = group // PIECES
        products, scales, sums = [None] * group, [None] * group, [None] * group
        gathered, pulls, spread = [None] * PIECES, [None] * PIECES, None
        for t in range(group + LAG_SUM):
            if t < group and t % 2 == 0:
                products[t : t + 2] = distances(near, far, ends[t], ends[t + 1])
            q = t // steps
            if t % steps == 0 and q < PIECES:
                gathered[q] = bond_gather(table[...], picks, start + q * piece, piece)
            q = (t - BOND_PULL) // steps
            if (t - BOND_PULL) % steps == 0 and 0 <= q < PIECES:
                pulls[q] = bond_pull(gathered[q], masks, start + q * piece, piece)
            q = t - LAG_SCALE
            if 0 <= q < group:
                i, j = ends[q]
                scales[q] = pair_scale(products[q], ratio[i], rho[pl.ds(j, 1), :])
            q = t - LAG_SUM
            if 0 <= q < group:
                sums[q] = pair_moments(moments, *ends[q], scales[q])
            q = (t - BOND_SPREAD) // steps
            if (t - BOND_SPREAD) % steps == 0 and 0 <= q < PIECES:
                part = bond_scatter(pulls[q], picks, masks, start + q * piece, piece)
                spread = part if spread is None else spread + part
        bond_sums[...] += spread
        for s, (i, j), (on_near, on_far) in zip(slots, ends, sums):
            weight = jnp.where(s < live, jnp.where(i == j, 0.5, 1.0), 0.0)
            acc[tile(i), :] += weight * on_near
            acc[tile(j), :] += weight * on_far
        return carry

    lax.fori_loop(0, ROUNDS, round_of, 0)
    for c in range(3):
        both = bond_sums[pl.ds(c * half, half), :]
        if first:
            both = both + bond_sums[pl.ds((3 + c) * half, half), :]
        for k in range(2):
            new = both[:, k * CA : (k + 1) * CA]
            if not first:
                new = new + bonded_before[c, pl.ds(k * half, half), :]
            bonded[c, pl.ds(k * half, half), :] = new


def edge_kernel(
    first,
    last,
    kick,
    tops,
    bottoms,
    slots,
    tally,
    lower,
    x_ref,
    v_ref,
    props,
    acc_in,
    bonded,
    upper_x,
    lower_x,
    upper_start,
    lower_start,
    *rest,
):
    *rest, stacks, moment_rows, near, far, moments, rho, acc = rest
    if last:
        ratio, state = rest
    elif first:
        x_out, v_out, to_upper, to_lower, ratio = rest
    else:
        ratio, x_out, v_out, to_upper, to_lower = rest
    clusters = x_ref.shape[1]
    facing = upper_x.shape[1]
    parts = position_parts(x_ref[0], x_ref[1], x_ref[2])
    far_stack(stacks, *parts)
    rho[...] = charge_ratio(props[0], props[1])
    for side, (hx, hp) in enumerate(((upper_x, upper_start), (lower_x, lower_start))):
        if first:
            fill_ratio(ratio, charge_ratio(hp[3], hp[4]), side * facing)
        near_stack(stacks, side * facing, *position_parts(hx[0], hx[1], hx[2]))
        moment_stack(moment_rows, side * facing, hx[0], hx[1], hx[2], hp[4])
    for c in range(clusters):
        fill_far(far, stacks, c)
    for c in range(2 * facing):
        fill_near(near, stacks, c)
        fill_moments(moments, moment_rows, c)
    acc[...] = acc_in[...]

    width = slots.shape[1]
    ends, weights = [], []
    for s in range(width):
        ends.append((slots[1, s], tops[0, slots[0, s]]))
        weights.append(jnp.where(s < tally[0, 0], 1.0, 0.0))
        ends.append((facing + lower[0, s], bottoms[0, lower[1, s]]))
        weights.append(jnp.where(s < lower[2, 0], 1.0, 0.0))
    count = len(ends)
    products, scales = [None] * count, [None] * count
    for t in range(count + EDGE_SUM):
        if t < count and t % 2 == 0:
            products[t : t + 2] = distances(near, far, ends[t], ends[t + 1])
        q = t - EDGE_SCALE
        if 0 <= q < count:
            j, i = ends[q]
            scales[q] = pair_scale(products[q], ratio[j], rho[pl.ds(i, 1), :])
        q = t - EDGE_SUM
        if 0 <= q < count:
            j, i = ends[q]
            total = moment_sums(moments[j], jnp.concatenate(scales[q], axis=1))
            acc[tile(i), :] += weights[q] * total

    def moment(k):
        high = acc[pl.ds(k, clusters, stride=ROWS), :]
        return high + acc[pl.ds(k + 4, clusters, stride=ROWS), :]

    mass = kick * props[2]
    g = props[1]
    count = moment(3)
    for c in range(3):
        force = g * (x_ref[c] * count - moment(c)) + bonded[c]
        v = v_ref[c] + mass * force
        if last:
            state[c] = x_ref[c]
            state[3 + c] = v
        else:
            v_out[c] = v
            x_out[c] = x_ref[c] + TIME_STEP * v
    if not last:
        pack_rows(tops, bottoms, x_out, to_upper, to_lower, 0, 3)


def pack_rows(tops, bottoms, source, to_upper, to_lower, base, count):
    for k in range(to_upper.shape[1]):
        i, j = tops[0, k], bottoms[0, k]
        up = [source[c, pl.ds(i, 1), :] for c in range(count)]
        down = [source[c, pl.ds(j, 1), :] for c in range(count)]
        for c in range(count):
            to_upper[base + c, pl.ds(k, 1), :] = up[c]
            to_lower[base + c, pl.ds(k, 1), :] = down[c]


def pack_kernel(*refs):
    ins, outs, scratch, sems = refs[:8], refs[8:13], refs[13:21], refs[21]
    props, to_upper, to_lower, index_rows, choice = outs
    copies = [
        pltpu.make_async_copy(source, target, sems.at[k])
        for k, (source, target) in enumerate(zip(ins, scratch))
    ]
    for copy in copies:
        copy.start()
    for copy in copies:
        copy.wait()
    tops, bottoms, levels, mates, x_ref, raw, slots, tally = scratch
    for c in range(3):
        for k in range(props.shape[1]):
            props[c, pl.ds(k, 1), :] = raw[pl.ds(c, 1), pl.ds(k * CA, CA)]
    pack_rows(tops, bottoms, x_ref, to_upper, to_lower, 0, 3)
    pack_rows(tops, bottoms, props, to_upper, to_lower, 3, 2)
    width = slots.shape[1]
    index_rows[...] = jnp.zeros_like(index_rows)
    index_rows[pl.ds(0, 2), pl.ds(0, width)] = slots[...]
    index_rows[pl.ds(2, 1), pl.ds(0, 1)] = tally[...]
    own = lax.axis_index("rep")
    mate = mates[own]
    near_mate = own + 1 - 2 * lax.rem(own, 2)
    row = (1, CA)
    ratio = jnp.full(row, levels[own], F32) / jnp.full(row, levels[mate], F32)
    choice[...] = jnp.zeros_like(choice)
    choice[pl.ds(0, 1), :] = jnp.full(row, jnp.where(mate == own, 1.0, 0.0), F32)
    choice[pl.ds(1, 1), :] = jnp.full(row, jnp.where(mate == near_mate, 1.0, 0.0), F32)
    choice[pl.ds(2, 1), :] = jnp.sqrt(ratio)


def local(
    atomic_locations,
    atomic_speeds,
    atomic_properties,
    resident_tile_members,
    resident_tile_tally,
    top_edge_groups,
    bottom_edge_groups,
    boundary_tile_slots,
    boundary_tile_tally,
    spring_links,
    thermal_levels,
    exchange_mate,
):
    atoms = atomic_locations.shape[2]
    clusters = atoms // CA
    facing = top_edge_groups.shape[1]
    shape = (3, clusters, CA)
    x = atomic_locations.reshape(shape)
    v = atomic_speeds.reshape(shape)
    pairs = resident_tile_members[:, 0]
    slots = boundary_tile_slots[:, 0]
    sds = jax.ShapeDtypeStruct
    params = pltpu.CompilerParams(vmem_limit_bytes=VMEM_LIMIT)

    props, to_upper, to_lower, index_rows, choice = pl.pallas_call(
        pack_kernel,
        out_shape=(
            sds(shape, F32),
            sds((5, facing, CA), F32),
            sds((5, facing, CA), F32),
            sds((ROWS, CA), jnp.int32),
            sds((ROWS, CA), F32),
        ),
        in_specs=[pl.BlockSpec(memory_space=pltpu.HBM)] * 8,
        out_specs=(VMEM,) * 5,
        scratch_shapes=[
            pltpu.SMEM(top_edge_groups.shape, jnp.int32),
            pltpu.SMEM(bottom_edge_groups.shape, jnp.int32),
            pltpu.SMEM(thermal_levels.shape, F32),
            pltpu.SMEM(exchange_mate.shape, jnp.int32),
            pltpu.VMEM(shape, F32),
            pltpu.VMEM(atomic_properties.shape, F32),
            pltpu.VMEM(slots.shape, jnp.int32),
            pltpu.VMEM(boundary_tile_tally.shape, jnp.int32),
            pltpu.SemaphoreType.DMA((8,)),
        ],
        compiler_params=params,
        name="pack",
    )(
        top_edge_groups,
        bottom_edge_groups,
        thermal_levels,
        exchange_mate,
        x,
        atomic_properties,
        slots,
        boundary_tile_tally,
    )
    upper_start = shifted(to_lower, "dom", -1)
    lower_start = shifted(to_upper, "dom", 1)
    lower = shifted(index_rows, "dom", 1)

    def scratch(sources):
        return [
            pltpu.VMEM((4, clusters * ROWS, CA), F32),
            pltpu.VMEM((clusters * ROWS, CA), F32),
            pltpu.VMEM((sources, 2 * ROWS, CA), BF16),
            pltpu.VMEM((clusters, 2, 2 * ROWS, CA), BF16),
            pltpu.VMEM((sources, 2 * ROWS, CA), BF16),
            pltpu.VMEM((clusters, CA), F32),
        ]

    bonds = spring_links.shape[1]
    kept = (
        sds((2, 2 * CA, bonds), BF16),
        sds((2, clusters // 2, bonds), BF16),
        sds((clusters, CA, CA), F32),
    )

    def local_call(first):
        sums = (sds((clusters * ROWS, CA), F32), sds(shape, F32))
        rows = 3 * clusters if first else 3 * clusters // 2
        return pl.pallas_call(
            functools.partial(local_kernel, first),
            out_shape=sums + kept if first else sums,
            in_specs=[SMEM] * 2 + [VMEM] * (3 if first else 7),
            out_specs=(VMEM,) * (5 if first else 2),
            scratch_shapes=scratch(clusters)
            + [
                pltpu.VMEM((rows, 2 * CA), BF16),
                pltpu.VMEM((rows, 2 * CA), F32),
            ],
            compiler_params=params,
            cost_estimate=pl.CostEstimate(
                flops=2_000_000_000, bytes_accessed=1_000_000, transcendentals=2_000_000
            ),
            name="resident",
        )

    def edge_call(first, last, kick):
        if last:
            outs = (sds((6, clusters, CA), F32),)
        else:
            outs = (sds(shape, F32),) * 2 + (sds((3, facing, CA), F32),) * 2
        if first:
            outs += (sds((2 * facing, CA, CA), F32),)
        return pl.pallas_call(
            functools.partial(edge_kernel, first, last, kick),
            out_shape=outs,
            in_specs=[SMEM] * 5 + [VMEM] * (9 if first else 10),
            out_specs=(VMEM,) * len(outs),
            scratch_shapes=scratch(2 * facing) + [pltpu.VMEM((clusters * ROWS, CA), F32)],
            compiler_params=params,
            cost_estimate=pl.CostEstimate(
                flops=1_000_000_000, bytes_accessed=1_000_000, transcendentals=2_000_000
            ),
            name="edges",
        )

    halo_ratio = ()
    upper_x, lower_x = upper_start, lower_start
    for step in range(STEPS + 1):
        if step == 0:
            acc, bonded, *static = local_call(True)(
                pairs, resident_tile_tally, x, props, spring_links
            )
        else:
            acc, bonded = local_call(False)(
                pairs, resident_tile_tally, x, props, x_before, bonded, *static
            )
        last = step == STEPS
        kick = TIME_STEP * (0.5 if step == 0 or last else 1.0)
        results = edge_call(step == 0, last, kick)(
            top_edge_groups,
            bottom_edge_groups,
            slots,
            boundary_tile_tally,
            lower,
            x,
            v,
            props,
            acc,
            bonded,
            upper_x,
            lower_x,
            upper_start,
            lower_start,
            *halo_ratio,
        )
        if last:
            (state,) = results
        else:
            x_before = x
            x, v, to_upper, to_lower, *new_ratio = results
            halo_ratio = halo_ratio or new_ratio
            upper_x = shifted(to_lower, "dom", -1)
            lower_x = shifted(to_upper, "dom", 1)

    keep, near_mate, ratio = choice[0] > 0.5, choice[1] > 0.5, choice[2]

    def chosen(own, one, two):
        return jnp.where(keep, own, jnp.where(near_mate, one, two))

    out = (3, 1, atoms)
    new = chosen(state, swapped(state, "rep", 0), swapped(state, "rep", 1))
    return new[:3].reshape(out), (new[3:] * ratio).reshape(out)


def solution(mesh):
    placed = (
        P(None, "rep", "dom"),
        P(None, "rep", "dom"),
        P(None, "dom"),
        P(None, "rep", "dom"),
        P("rep", "dom"),
        P("rep", "dom"),
        P("rep", "dom"),
        P(None, "rep", "dom"),
        P("rep", "dom"),
        P(None, "dom"),
        P(),
        P(),
    )
    return jax.shard_map(
        local,
        mesh=mesh,
        in_specs=placed,
        out_specs=(P(None, "rep", "dom"), P(None, "rep", "dom")),
        check_vma=False,
    )
```

profile of v0, /device:TPU:1, one launch (start us, length us, event | category | flops | bytes accessed | tf_op | source)
XLA Modules:
  0.0 64.0 jit_solution(6029932324971450950)
XLA Ops:
  1.3 0.9 %copy-done = f32[3,1,8192]{2,1,0:T(1,128)S(1)} copy-done((f32[3,1,8192]{2,1,0:T(1,128)S(1)}, f32[3,1,8192]{2,1,0:T(1,128)}, u32[]{:S(2)}) %copy-start) | copy-done | bytes 98328
  2.2 0.9 %copy-done.2 = f32[3,8192]{1,0:T(4,128)S(1)} copy-done((f32[3,8192]{1,0:T(4,128)S(1)}, f32[3,8192]{1,0:T(4,128)}, u32[]{:S(2)}) %copy-start.2) | copy-done | bytes 98328
  3.1 0.7 %copy-done.3 = s32[2,1,32]{2,1,0:T(1,128)S(1)} copy-done((s32[2,1,32]{2,1,0:T(1,128)S(1)}, s32[2,1,32]{2,1,0:T(1,128)}, u32[]{:S(2)}) %copy-start.3) | copy-done | bytes 280
  3.8 0.7 %copy-done.5 = s32[1,32]{1,0:T(1,128)S(1)} copy-done((s32[1,32]{1,0:T(1,128)S(1)}, s32[1,32]{1,0:T(1,128)}, u32[]{:S(2)}) %copy-start.5) | copy-done | bytes 152
  4.4 0.7 %copy-done.6 = s32[1,32]{1,0:T(1,128)S(1)} copy-done((s32[1,32]{1,0:T(1,128)S(1)}, s32[1,32]{1,0:T(1,128)}, u32[]{:S(2)}) %copy-start.6) | copy-done | bytes 152
  5.1 0.7 %copy-done.9 = f32[32]{0:T(128)S(1)} copy-done((f32[32]{0:T(128)S(1)}, f32[32]{0:T(128)}, u32[]{:S(2)}) %copy-start.9) | copy-done | bytes 152
  5.7 0.7 %copy-done.10 = s32[32]{0:T(128)S(1)} copy-done((s32[32]{0:T(128)S(1)}, s32[32]{0:T(128)}, u32[]{:S(2)}) %copy-start.10) | copy-done | bytes 152
  6.4 0.9 %pack.1 = (f32[3,64,128]{2,1,0:T(8,128)S(1)}, f32[5,32,128]{2,1,0:T(8,128)S(1)}, f32[5,32,128]{2,1,0:T(8,128)S(1)}, s32[8,128]{1,0:T(8,128)S(1)}, f32[8,128]{1,0:T(8,128)S(1)}) custom-call(s32[1,32]{1,0:T(1,128)S(1)} %copy-done.5, s32[1,32]{1,0:T(1,128)S(1)} %copy-done.6, f32[32]{0:T(128)S(1)} %copy-done.9, s32[32]{0:T(128)S(1)} %copy-done.10, ...), custom_call_target="tpu_custom_call" | custom-call | tf_op jit(solution)/shard_map/pack/pallas_call | solution.py:453
  7.3 2.1 %collective-permute-start = (s32[8,128]{1,0:T(8,128)S(1)}, s32[8,128]{1,0:T(8,128)S(1)}, u32[]{:S(2)}, u32[]{:S(2)}) collective-permute-start(s32[8,128]{1,0:T(8,128)S(1)} %get-tuple-element.26), channel_id=1, source_target_pairs={{0,1},{1,2},{2,3},{3,4},{4,5},{5,6},{6,7},{7,0},{8,9},{9,10},{10,1... | collective-permute-start | bytes 12296 | tf_op jit(solution)/shard_map/ppermute | solution.py:35
  9.4 2.7 %collective-permute-start.1 = (f32[5,32,128]{2,1,0:T(8,128)S(1)}, f32[5,32,128]{2,1,0:T(8,128)S(1)}, u32[]{:S(2)}, u32[]{:S(2)}) collective-permute-start(f32[5,32,128]{2,1,0:T(8,128)S(1)} %get-tuple-element.30), channel_id=1, source_target_pairs={{0,7},{1,0},{2,1},{3,2},{4,3},{5,4},{6,5},{7,6},{8,15},{9,8},{10,9... | collective-permute-start | bytes 245768 | tf_op jit(solution)/shard_map/ppermute | solution.py:35
  12.1 0.0 collective-permute-start.2
  12.8 0.0 copy-start.7
  12.8 0.7 %copy-done.7 = s32[2,1,64]{2,1,0:T(1,128)S(1)} copy-done((s32[2,1,64]{2,1,0:T(1,128)S(1)}, s32[2,1,64]{2,1,0:T(1,128)}, u32[]{:S(2)}) %copy-start.7) | copy-done | bytes 536
  13.5 0.8 %copy-done.12 = s32[2,4096]{1,0:T(2,128)S(1)} copy-done((s32[2,4096]{1,0:T(2,128)S(1)}, s32[2,4096]{1,0:T(2,128)}, u32[]{:S(2)}) %copy-start.12) | copy-done | bytes 32792
  14.3 7.4 %resident.3 = (f32[512,128]{1,0:T(8,128)S(1)}, f32[3,64,128]{2,1,0:T(8,128)S(1)}, bf16[2,256,4096]{2,1,0:T(8,128)(2,1)S(1)}, bf16[2,32,4096]{2,1,0:T(8,128)(2,1)S(1)}, f32[64,128,128]{2,1,0:T(8,128)S(1)}) custom-call(s32[2,64]{1,0:T(2,128)S(1)} %bitcast.20, s32[1,1]{1,0:T(1,128)S(6)} %copy.18.tally, f32[3,64,128]{2,1,0:T(8,128)S(1)} %bitcast.13, ...), custom_call_target="tpu_custom_call" | custom-call | flops 2000000000 | bytes 1000000 | tf_op jit(solution)/shard_map/resident/pallas_call | solution.py:552
  21.6 0.0 collective-permute-done.lower
  21.7 4.1 %edges.3 = (f32[3,64,128]{2,1,0:T(8,128)S(1)}, f32[3,64,128]{2,1,0:T(8,128)S(1)}, f32[3,32,128]{2,1,0:T(8,128)S(1)}, f32[3,32,128]{2,1,0:T(8,128)S(1)}, f32[64,128,128]{2,1,0:T(8,128)S(1)}) custom-call(s32[1,32]{1,0:T(1,128)S(1)} %copy-done.5, s32[1,32]{1,0:T(1,128)S(1)} %copy-done.6, s32[2,32]{1,0:T(2,128)S(1)} %bitcast.17, s32[1,1]{1,0:T(1,128)S(6)} %copy.19.refs_7_.tally, ...), custom_call_target="tpu_custom_call" | custom-call | flops 1000000000 | bytes 1000000 | tf_op jit(solution)/shard_map/edges/pallas_call | solution.py:561
  25.7 3.7 %collective-permute-start.3 = (f32[3,32,128]{2,1,0:T(8,128)S(1)}, f32[3,32,128]{2,1,0:T(8,128)S(1)}, u32[]{:S(2)}, u32[]{:S(2)}) collective-permute-start(f32[3,32,128]{2,1,0:T(8,128)S(1)} %get-tuple-element.39), channel_id=1, source_target_pairs={{0,7},{1,0},{2,1},{3,2},{4,3},{5,4},{6,5},{7,6},{8,15},{9,8},{10,9... | collective-permute-start | bytes 147464 | tf_op jit(solution)/shard_map/ppermute | solution.py:35
  29.4 0.0 collective-permute-start.4
  29.4 5.7 %resident.4 = (f32[512,128]{1,0:T(8,128)S(1)}, f32[3,64,128]{2,1,0:T(8,128)S(1)}) custom-call(s32[2,64]{1,0:T(2,128)S(1)} %bitcast.21, s32[1,1]{1,0:T(1,128)S(6)} %copy.18.tally, f32[3,64,128]{2,1,0:T(8,128)S(1)} %get-tuple-element.32.x_ref.rest_0_, f32[3,64,128]{2,1,0:T(8,128)S(1)} %get-tuple-element.27.props, f32[3,64,128]{2,1,0:T(8,128)S(1)} %bitcast.15, ...), custom_call_target="tpu_custom_call" | custom-call | flops 2000000000 | bytes 1000000 | tf_op jit(solution)/shard_map/resident/pallas_call | solution.py:556
  35.2 0.0 copy-start.8
  35.2 0.0 collective-permute-done.4.lower_x
  35.2 3.0 %edges.4 = (f32[3,64,128]{2,1,0:T(8,128)S(1)}, f32[3,64,128]{2,1,0:T(8,128)S(1)}, f32[3,32,128]{2,1,0:T(8,128)S(1)}, f32[3,32,128]{2,1,0:T(8,128)S(1)}) custom-call(s32[1,32]{1,0:T(1,128)S(1)} %copy-done.5, s32[1,32]{1,0:T(1,128)S(1)} %copy-done.6, s32[2,32]{1,0:T(2,128)S(1)} %bitcast.18, s32[1,1]{1,0:T(1,128)S(6)} %copy.19.refs_7_.tally, ...), custom_call_target="tpu_custom_call" | custom-call | flops 1000000000 | bytes 1000000 | tf_op jit(solution)/shard_map/edges/pallas_call | solution.py:561
  38.2 3.6 %collective-permute-start.5 = (f32[3,32,128]{2,1,0:T(8,128)S(1)}, f32[3,32,128]{2,1,0:T(8,128)S(1)}, u32[]{:S(2)}, u32[]{:S(2)}) collective-permute-start(f32[3,32,128]{2,1,0:T(8,128)S(1)} %get-tuple-element.46), channel_id=1, source_target_pairs={{0,7},{1,0},{2,1},{3,2},{4,3},{5,4},{6,5},{7,6},{8,15},{9,8},{10,9... | collective-permute-start | bytes 147464 | tf_op jit(solution)/shard_map/ppermute | solution.py:35
  41.9 0.0 collective-permute-start.6
  41.9 5.7 %resident.5 = (f32[512,128]{1,0:T(8,128)S(1)}, f32[3,64,128]{2,1,0:T(8,128)S(1)}) custom-call(s32[2,64]{1,0:T(2,128)S(1)} %bitcast.22, s32[1,1]{1,0:T(1,128)S(6)} %copy.18.tally, f32[3,64,128]{2,1,0:T(8,128)S(1)} %get-tuple-element.42.x_ref, f32[3,64,128]{2,1,0:T(8,128)S(1)} %get-tuple-element.27.props, f32[3,64,128]{2,1,0:T(8,128)S(1)} %get-tuple-element.32.x_ref.rest_0_, ...), custom_call_target="tpu_custom_call" | custom-call | flops 2000000000 | bytes 1000000 | tf_op jit(solution)/shard_map/resident/pallas_call | solution.py:556
  47.6 0.0 collective-permute-done.5.upper_x
  47.6 2.9 %edges.5 = f32[6,64,128]{2,1,0:T(8,128)S(1)} custom-call(s32[1,32]{1,0:T(1,128)S(1)} %copy-done.5, s32[1,32]{1,0:T(1,128)S(1)} %copy-done.6, s32[2,32]{1,0:T(2,128)S(1)} %bitcast.19, s32[1,1]{1,0:T(1,128)S(6)} %copy.19.refs_7_.tally, s32[8,128]{1,0:T(8,128)S(1)} %collective-permute-done.lower, f32[3,64,128]{2,1,0:T(8,128)S(1)} %get-tuple-element.42.x_ref, ...), custom_call_target="tpu_custom_call" | custom-call | flops 1000000000 | bytes 1000000 | tf_op jit(solution)/shard_map/edges/pallas_call | solution.py:561
  50.5 7.3 %collective-permute-start.8 = (f32[6,64,128]{2,1,0:T(8,128)S(1)}, f32[6,64,128]{2,1,0:T(8,128)S(1)}, u32[]{:S(2)}, u32[]{:S(2)}) collective-permute-start(f32[6,64,128]{2,1,0:T(8,128)S(1)} %edges.5), channel_id=1, source_target_pairs={{8,16},{16,8},{24,32},{32,24},{40,48},{48,40},{56,64},{64,56},{72,... | collective-permute-start | bytes 589832 | tf_op jit(solution)/shard_map/ppermute | solution.py:43
  57.8 0.1 collective-permute-start.7
  57.9 5.3 %collective-permute-done.8 = f32[6,64,128]{2,1,0:T(8,128)S(1)} collective-permute-done((f32[6,64,128]{2,1,0:T(8,128)S(1)}, f32[6,64,128]{2,1,0:T(8,128)S(1)}, u32[]{:S(2)}, u32[]{:S(2)}) %collective-permute-start.8) | collective-permute-done | bytes 196640 | tf_op jit(solution)/shard_map/ppermute | solution.py:43
  63.3 0.7 %slice_multiply_fusion = (f32[3,64,128]{2,1,0:T(8,128)}, f32[3,64,128]{2,1,0:T(8,128)}) fusion(f32[6,64,128]{2,1,0:T(8,128)S(1)} %select_select_fusion, f32[128]{0:T(128)S(1)} %slice_bitcast_fusion), kind=kLoop, calls=%fused_computation.1 | loop fusion | flops 24576 | bytes 393728 | tf_op jit(solution)/shard_map/mul | solution.py:594
  (23 shorter events, 0.1 us)
Async XLA Ops:
  0.6 21.0 %copy-start.4 = (s32[2,1,32]{2,1,0:T(1,128)S(1)}, s32[2,1,32]{2,1,0:T(1,128)}, u32[]{:S(2)}) copy-start(s32[2,1,32]{2,1,0:T(1,128)} %param.19) | copy-start | bytes 772
  1.3 0.9 %copy-start = (f32[3,1,8192]{2,1,0:T(1,128)S(1)}, f32[3,1,8192]{2,1,0:T(1,128)}, u32[]{:S(2)}) copy-start(f32[3,1,8192]{2,1,0:T(1,128)} %param.12) | copy-start | bytes 294916
  2.2 0.9 %copy-start.2 = (f32[3,8192]{1,0:T(4,128)S(1)}, f32[3,8192]{1,0:T(4,128)}, u32[]{:S(2)}) copy-start(f32[3,8192]{1,0:T(4,128)} %refs_5_.1) | copy-start | bytes 294916
  3.1 0.7 %copy-start.3 = (s32[2,1,32]{2,1,0:T(1,128)S(1)}, s32[2,1,32]{2,1,0:T(1,128)}, u32[]{:S(2)}) copy-start(s32[2,1,32]{2,1,0:T(1,128)} %param.19) | copy-start | bytes 772
  3.8 0.7 %copy-start.5 = (s32[1,32]{1,0:T(1,128)S(1)}, s32[1,32]{1,0:T(1,128)}, u32[]{:S(2)}) copy-start(s32[1,32]{1,0:T(1,128)} %tops.5) | copy-start | bytes 388
  4.4 0.7 %copy-start.6 = (s32[1,32]{1,0:T(1,128)S(1)}, s32[1,32]{1,0:T(1,128)}, u32[]{:S(2)}) copy-start(s32[1,32]{1,0:T(1,128)} %bottoms.5) | copy-start | bytes 388
  5.1 0.7 %copy-start.9 = (f32[32]{0:T(128)S(1)}, f32[32]{0:T(128)}, u32[]{:S(2)}) copy-start(f32[32]{0:T(128)} %refs_2_.1) | copy-start | bytes 388
  5.7 0.7 %copy-start.10 = (s32[32]{0:T(128)S(1)}, s32[32]{0:T(128)}, u32[]{:S(2)}) copy-start(s32[32]{0:T(128)} %refs_3_.1) | copy-start | bytes 388
  6.4 15.3 %copy-start.1 = (f32[3,1,8192]{2,1,0:T(1,128)S(1)}, f32[3,1,8192]{2,1,0:T(1,128)}, u32[]{:S(2)}) copy-start(f32[3,1,8192]{2,1,0:T(1,128)} %param.12) | copy-start | bytes 294916
  6.4 15.3 %copy-start.11 = (f32[3,1,8192]{2,1,0:T(1,128)S(1)}, f32[3,1,8192]{2,1,0:T(1,128)}, u32[]{:S(2)}) copy-start(f32[3,1,8192]{2,1,0:T(1,128)} %param.13) | copy-start | bytes 294916
  7.3 14.3 %collective-permute-start = (s32[8,128]{1,0:T(8,128)S(1)}, s32[8,128]{1,0:T(8,128)S(1)}, u32[]{:S(2)}, u32[]{:S(2)}) collective-permute-start(s32[8,128]{1,0:T(8,128)S(1)} %get-tuple-element.26), channel_id=1, source_target_pairs={{0,1},{1,2},{2,3},{3,4},{4,5},{5,6},{6,7},{7,0},{8,9},{9,10},{10,1... | collective-permute-start | bytes 12296 | tf_op jit(solution)/shard_map/ppermute | solution.py:35
  9.4 12.2 %collective-permute-start.1 = (f32[5,32,128]{2,1,0:T(8,128)S(1)}, f32[5,32,128]{2,1,0:T(8,128)S(1)}, u32[]{:S(2)}, u32[]{:S(2)}) collective-permute-start(f32[5,32,128]{2,1,0:T(8,128)S(1)} %get-tuple-element.30), channel_id=1, source_target_pairs={{0,7},{1,0},{2,1},{3,2},{4,3},{5,4},{6,5},{7,6},{8,15},{9,8},{10,9... | collective-permute-start | bytes 245768 | tf_op jit(solution)/shard_map/ppermute | solution.py:35
  12.1 9.5 %collective-permute-start.2 = (f32[5,32,128]{2,1,0:T(8,128)S(1)}, f32[5,32,128]{2,1,0:T(8,128)S(1)}, u32[]{:S(2)}, u32[]{:S(2)}) collective-permute-start(f32[5,32,128]{2,1,0:T(8,128)S(1)} %get-tuple-element.31), channel_id=1, source_target_pairs={{0,1},{1,2},{2,3},{3,4},{4,5},{5,6},{6,7},{7,0},{8,9},{9,10},{10,1... | collective-permute-start | bytes 245768 | tf_op jit(solution)/shard_map/ppermute | solution.py:35
  12.8 0.7 %copy-start.7 = (s32[2,1,64]{2,1,0:T(1,128)S(1)}, s32[2,1,64]{2,1,0:T(1,128)}, u32[]{:S(2)}) copy-start(s32[2,1,64]{2,1,0:T(1,128)} %param.15) | copy-start | bytes 1540
  13.5 0.8 %copy-start.12 = (s32[2,4096]{1,0:T(2,128)S(1)}, s32[2,4096]{1,0:T(2,128)}, u32[]{:S(2)}) copy-start(s32[2,4096]{1,0:T(2,128)} %rest_0_.1) | copy-start | bytes 98308
  25.7 9.4 %collective-permute-start.3 = (f32[3,32,128]{2,1,0:T(8,128)S(1)}, f32[3,32,128]{2,1,0:T(8,128)S(1)}, u32[]{:S(2)}, u32[]{:S(2)}) collective-permute-start(f32[3,32,128]{2,1,0:T(8,128)S(1)} %get-tuple-element.39), channel_id=1, source_target_pairs={{0,7},{1,0},{2,1},{3,2},{4,3},{5,4},{6,5},{7,6},{8,15},{9,8},{10,9... | collective-permute-start | bytes 147464 | tf_op jit(solution)/shard_map/ppermute | solution.py:35
  29.4 5.8 %collective-permute-start.4 = (f32[3,32,128]{2,1,0:T(8,128)S(1)}, f32[3,32,128]{2,1,0:T(8,128)S(1)}, u32[]{:S(2)}, u32[]{:S(2)}) collective-permute-start(f32[3,32,128]{2,1,0:T(8,128)S(1)} %get-tuple-element.40), channel_id=1, source_target_pairs={{0,1},{1,2},{2,3},{3,4},{4,5},{5,6},{6,7},{7,0},{8,9},{9,10},{10,1... | collective-permute-start | bytes 147464 | tf_op jit(solution)/shard_map/ppermute | solution.py:35
  35.2 6.7 %copy-start.8 = (s32[2,1,64]{2,1,0:T(1,128)S(1)}, s32[2,1,64]{2,1,0:T(1,128)}, u32[]{:S(2)}) copy-start(s32[2,1,64]{2,1,0:T(1,128)} %param.15) | copy-start | bytes 1540
  38.2 9.4 %collective-permute-start.5 = (f32[3,32,128]{2,1,0:T(8,128)S(1)}, f32[3,32,128]{2,1,0:T(8,128)S(1)}, u32[]{:S(2)}, u32[]{:S(2)}) collective-permute-start(f32[3,32,128]{2,1,0:T(8,128)S(1)} %get-tuple-element.46), channel_id=1, source_target_pairs={{0,7},{1,0},{2,1},{3,2},{4,3},{5,4},{6,5},{7,6},{8,15},{9,8},{10,9... | collective-permute-start | bytes 147464 | tf_op jit(solution)/shard_map/ppermute | solution.py:35
  41.9 5.8 %collective-permute-start.6 = (f32[3,32,128]{2,1,0:T(8,128)S(1)}, f32[3,32,128]{2,1,0:T(8,128)S(1)}, u32[]{:S(2)}, u32[]{:S(2)}) collective-permute-start(f32[3,32,128]{2,1,0:T(8,128)S(1)} %get-tuple-element.47), channel_id=1, source_target_pairs={{0,1},{1,2},{2,3},{3,4},{4,5},{5,6},{6,7},{7,0},{8,9},{9,10},{10,1... | collective-permute-start | bytes 147464 | tf_op jit(solution)/shard_map/ppermute | solution.py:35
  50.5 12.7 %collective-permute-start.8 = (f32[6,64,128]{2,1,0:T(8,128)S(1)}, f32[6,64,128]{2,1,0:T(8,128)S(1)}, u32[]{:S(2)}, u32[]{:S(2)}) collective-permute-start(f32[6,64,128]{2,1,0:T(8,128)S(1)} %edges.5), channel_id=1, source_target_pairs={{8,16},{16,8},{24,32},{32,24},{40,48},{48,40},{56,64},{64,56},{72,... | collective-permute-start | bytes 589832 | tf_op jit(solution)/shard_map/ppermute | solution.py:43
  57.8 5.4 %collective-permute-start.7 = (f32[6,64,128]{2,1,0:T(8,128)S(1)}, f32[6,64,128]{2,1,0:T(8,128)S(1)}, u32[]{:S(2)}, u32[]{:S(2)}) collective-permute-start(f32[6,64,128]{2,1,0:T(8,128)S(1)} %edges.5), channel_id=1, source_target_pairs={{0,8},{8,0},{16,24},{24,16},{32,40},{40,32},{48,56},{56,48},{64,72... | collective-permute-start | bytes 589832 | tf_op jit(solution)/shard_map/ppermute | solution.py:43
where the time goes:
time: 65.1 us; the launch traced here: 64 us
  Pallas kernels  29.7 us (46%)
  starting transfers between devices  19.5 us (30%)
  local copies, waits for them, and re-layouts  6.54 us (10%)
  waiting for transfers between devices  5.35 us (8%)
  between operations  2.16 us (3%)
  other arithmetic  0.73 us (1%)
    ppermute x7, starting transfers between devices, shifted(): lax.ppermute(shard, axis, [(i, (i + by) % devices) for i in range(devices)])  12.1 us
    pallas_call x2, Pallas kernels, local(): local_call(False)  11.4 us
    pallas_call x3, Pallas kernels, local(): edge_call(step == 0, last, kick)  9.97 us
    ppermute x2, starting transfers between devices, swapped(): return lax.ppermute(shard, axis, pairs)  7.39 us
    pallas_call x1, Pallas kernels, local(): local_call(True)(pairs, resident_tile_tally, x, props, spring_links)  7.36 us
    unnamed x26, local copies, waits for them, and re-layouts  6.54 us
    ppermute x2, waiting for transfers between devices, swapped(): return lax.ppermute(shard, axis, pairs)  5.34 us
  transfers between devices with their start and end apart: 9, of which 1 were waited for; matrix products, arithmetic and copies ran while one was open for 0% of the time, Pallas kernels for 29%

commit v1 on v0

--- a/solution.py
+++ b/solution.py
@@ -16,8 +16,8 @@
 BF16 = jnp.bfloat16
 LOG2E = 1.4426950408889634
 ROWS = 8
-ROUNDS = 4
-PIECES = 4
+ROUNDS = 1
+PIECES = 16
 LAG_SCALE = 3
 LAG_SUM = 6
 EDGE_SCALE = 3
@@ -25,6 +25,7 @@
 BOND_PULL = 2
 BOND_SPREAD = 4
 VMEM_LIMIT = 20 << 20
+PACK_LIMIT = 60 << 20
 
 SMEM = pl.BlockSpec(memory_space=pltpu.SMEM)
 VMEM = pl.BlockSpec(memory_space=pltpu.VMEM)
@@ -393,18 +394,9 @@
             to_lower[base + c, pl.ds(k, 1), :] = down[c]
 
 
-def pack_kernel(*refs):
-    ins, outs, scratch, sems = refs[:8], refs[8:13], refs[13:21], refs[21]
-    props, to_upper, to_lower, index_rows, choice = outs
-    copies = [
-        pltpu.make_async_copy(source, target, sems.at[k])
-        for k, (source, target) in enumerate(zip(ins, scratch))
-    ]
-    for copy in copies:
-        copy.start()
-    for copy in copies:
-        copy.wait()
-    tops, bottoms, levels, mates, x_ref, raw, slots, tally = scratch
+def pack_kernel(
+    tops, bottoms, levels, mates, x_ref, raw, slots, tally, props, to_upper, to_lower, index_rows, choice
+):
     for c in range(3):
         for k in range(props.shape[1]):
             props[c, pl.ds(k, 1), :] = raw[pl.ds(c, 1), pl.ds(k * CA, CA)]
@@ -459,20 +451,9 @@
             sds((ROWS, CA), jnp.int32),
             sds((ROWS, CA), F32),
         ),
-        in_specs=[pl.BlockSpec(memory_space=pltpu.HBM)] * 8,
+        in_specs=[SMEM] * 4 + [VMEM] * 4,
         out_specs=(VMEM,) * 5,
-        scratch_shapes=[
-            pltpu.SMEM(top_edge_groups.shape, jnp.int32),
-            pltpu.SMEM(bottom_edge_groups.shape, jnp.int32),
-            pltpu.SMEM(thermal_levels.shape, F32),
-            pltpu.SMEM(exchange_mate.shape, jnp.int32),
-            pltpu.VMEM(shape, F32),
-            pltpu.VMEM(atomic_properties.shape, F32),
-            pltpu.VMEM(slots.shape, jnp.int32),
-            pltpu.VMEM(boundary_tile_tally.shape, jnp.int32),
-            pltpu.SemaphoreType.DMA((8,)),
-        ],
-        compiler_params=params,
+        compiler_params=pltpu.CompilerParams(vmem_limit_bytes=PACK_LIMIT),
         name="pack",
     )(
         top_edge_groups,

time: 65.1 us -> 60.9 us (0.935)
  local copies, waits for them, and re-layouts: 6.54 us -> 3.94 us
  Pallas kernels: 29.7 us -> 27.3 us
  other arithmetic: 0.73 us -> 1.5 us
    unnamed x26 -> x22, local copies, waits for them, and re-layouts: 6.54 us -> 3.25 us
    pallas_call x2, Pallas kernels: 11.4 us -> 9.41 us  [local(): local_call(False)]
    pallas_call x1, Pallas kernels: 7.36 us -> 6.04 us  [local(): local_call(True)(pairs, resident_tile_tally, x, props, spring_links)]
    pallas_call x1, Pallas kernels: 0.91 us -> 1.87 us  [local(): pl.pallas_call(pack_kernel, out_shape=(sds(shape, F32), sds((5, facing, C...]
    gt x1, other arithmetic: 0.01 us -> 0.77 us  [local(): keep, near_mate, ratio = (choice[0] > 0.5, choice[1] > 0.5, choice[2])]
    ppermute x2, starting transfers between devices: 7.39 us -> 8.09 us  [swapped(): return lax.ppermute(shard, axis, pairs)]
    mul x1, local copies, waits for them, and re-layouts: 0.01 us -> 0.69 us  [local(): return (new[:3].reshape(out), (new[3:] * ratio).reshape(out))]
    ppermute x2, waiting for transfers between devices: 5.34 us -> 4.66 us  [swapped(): return lax.ppermute(shard, axis, pairs)]
  transfers between devices with their start and end apart: 9 -> 9, of which waited for: 1 -> 3; matrix products, arithmetic and copies ran while one was open for 0% -> 2% of each run, Pallas kernels for 29% -> 26%
where the time goes in v1:
time: 60.9 us; the launch traced here: 60.2 us
  Pallas kernels  27.3 us (45%)
  starting transfers between devices  20 us (33%)
  waiting for transfers between devices  5.31 us (9%)
  local copies, waits for them, and re-layouts  3.94 us (6%)
  between operations  2.16 us (4%)
  other arithmetic  1.5 us (2%)
    ppermute x7, starting transfers between devices, shifted(): lax.ppermute(shard, axis, [(i, (i + by) % devices) for i in range(devices)])  11.9 us
    pallas_call x3, Pallas kernels, local(): edge_call(step == 0, last, kick)  9.96 us
    pallas_call x2, Pallas kernels, local(): local_call(False)  9.41 us
    ppermute x2, starting transfers between devices, swapped(): return lax.ppermute(shard, axis, pairs)  8.09 us
    pallas_call x1, Pallas kernels, local(): local_call(True)(pairs, resident_tile_tally, x, props, spring_links)  6.04 us
    ppermute x2, waiting for transfers between devices, swapped(): return lax.ppermute(shard, axis, pairs)  4.66 us
    unnamed x22, local copies, waits for them, and re-layouts  3.25 us
    pallas_call x1, Pallas kernels, local(): pl.pallas_call(pack_kernel, out_shape=(sds(shape, F32), sds((5, facing, C...  1.87 us
  transfers between devices with their start and end apart: 9, of which 3 were waited for; matrix products, arithmetic and copies ran while one was open for 2% of the time, Pallas kernels for 26%

profile of v1, /device:TPU:1, one launch (start us, length us, event | category | flops | bytes accessed | tf_op | source)
XLA Modules:
  0.0 60.2 jit_solution(10820064395262683166)
XLA Ops:
  0.7 0.0 copy-start.3
  1.4 1.9 %pack.1 = (f32[3,64,128]{2,1,0:T(8,128)}, f32[5,32,128]{2,1,0:T(8,128)}, f32[5,32,128]{2,1,0:T(8,128)}, s32[8,128]{1,0:T(8,128)}, f32[8,128]{1,0:T(8,128)}) custom-call(s32[1,32]{1,0:T(1,128)} %tops.7, s32[1,32]{1,0:T(1,128)} %bottoms.7, f32[32]{0:T(128)} %levels.1, s32[32]{0:T(128)} %mates.1, f32[3,64,128]{2,1,0:T(8,128)} %bitcast.12, f32[3,8192]{1,0:T(4,128)} %raw.1, ...), custom_call_target="tpu_custom_call" | custom-call | tf_op jit(solution)/shard_map/pack/pallas_call | solution.py:445
  3.2 2.0 %collective-permute-start = (s32[8,128]{1,0:T(8,128)}, s32[8,128]{1,0:T(8,128)S(1)}, u32[]{:S(2)}, u32[]{:S(2)}) collective-permute-start(s32[8,128]{1,0:T(8,128)} %get-tuple-element.26), channel_id=1, source_target_pairs={{0,1},{1,2},{2,3},{3,4},{4,5},{5,6},{6,7},{7,0},{8,9},{9,10},{10,1... | collective-permute-start | bytes 12296 | tf_op jit(solution)/shard_map/ppermute | solution.py:36
  5.3 2.7 %collective-permute-start.1 = (f32[5,32,128]{2,1,0:T(8,128)}, f32[5,32,128]{2,1,0:T(8,128)S(1)}, u32[]{:S(2)}, u32[]{:S(2)}) collective-permute-start(f32[5,32,128]{2,1,0:T(8,128)} %get-tuple-element.30), channel_id=1, source_target_pairs={{0,7},{1,0},{2,1},{3,2},{4,3},{5,4},{6,5},{7,6},{8,15},{9,8},{10,9... | collective-permute-start | bytes 245768 | tf_op jit(solution)/shard_map/ppermute | solution.py:36
  8.0 0.0 collective-permute-start.2
  8.6 0.8 %compare_bitcast_fusion.1 = (pred[128]{0:T(512)(128)(4,1)S(1)}, pred[128]{0:T(512)(128)(4,1)S(1)}) fusion(f32[8,128]{1,0:T(8,128)} %get-tuple-element.25), kind=kLoop, calls=%fused_computation.3 | loop fusion | flops 256 | bytes 1280 | tf_op jit(solution)/shard_map/gt | solution.py:568
  9.4 0.9 %copy-done = f32[3,64,128]{2,1,0:T(8,128)S(1)} copy-done((f32[3,64,128]{2,1,0:T(8,128)S(1)}, f32[3,64,128]{2,1,0:T(8,128)}, u32[]{:S(2)}) %copy-start) | copy-done | bytes 98328
  10.3 0.9 %copy-done.2 = f32[3,1,8192]{2,1,0:T(1,128)S(1)} copy-done((f32[3,1,8192]{2,1,0:T(1,128)S(1)}, f32[3,1,8192]{2,1,0:T(1,128)}, u32[]{:S(2)}) %copy-start.2) | copy-done | bytes 98328
  11.2 0.7 %copy-done.7 = s32[2,1,64]{2,1,0:T(1,128)S(1)} copy-done((s32[2,1,64]{2,1,0:T(1,128)S(1)}, s32[2,1,64]{2,1,0:T(1,128)}, u32[]{:S(2)}) %copy-start.7) | copy-done | bytes 536
  11.9 0.8 %copy-done.10 = s32[2,4096]{1,0:T(2,128)S(1)} copy-done((s32[2,4096]{1,0:T(2,128)S(1)}, s32[2,4096]{1,0:T(2,128)}, u32[]{:S(2)}) %copy-start.10) | copy-done | bytes 32792
  12.6 6.0 %resident.3 = (f32[512,128]{1,0:T(8,128)S(1)}, f32[3,64,128]{2,1,0:T(8,128)S(1)}, bf16[2,256,4096]{2,1,0:T(8,128)(2,1)S(1)}, bf16[2,32,4096]{2,1,0:T(8,128)(2,1)S(1)}, f32[64,128,128]{2,1,0:T(8,128)S(1)}) custom-call(s32[2,64]{1,0:T(2,128)S(1)} %bitcast.20, s32[1,1]{1,0:T(1,128)S(6)} %copy.18.tally, f32[3,64,128]{2,1,0:T(8,128)S(1)} %bitcast.13, ...), custom_call_target="tpu_custom_call" | custom-call | flops 2000000000 | bytes 1000000 | tf_op jit(solution)/shard_map/resident/pallas_call | solution.py:533
  18.7 0.0 collective-permute-done.lower
  18.7 0.0 collective-permute-done.1.upper_x.upper_start
  18.7 0.0 collective-permute-done.2.lower_x.lower_start
  18.7 4.1 %edges.3 = (f32[3,64,128]{2,1,0:T(8,128)S(1)}, f32[3,64,128]{2,1,0:T(8,128)S(1)}, f32[3,32,128]{2,1,0:T(8,128)S(1)}, f32[3,32,128]{2,1,0:T(8,128)S(1)}, f32[64,128,128]{2,1,0:T(8,128)S(1)}) custom-call(s32[1,32]{1,0:T(1,128)S(1)} %copy-done.5, s32[1,32]{1,0:T(1,128)S(1)} %copy-done.6, s32[2,32]{1,0:T(2,128)S(1)} %bitcast.17, s32[1,1]{1,0:T(1,128)S(6)} %copy.19.tally, ...), custom_call_target="tpu_custom_call" | custom-call | flops 1000000000 | bytes 1000000 | tf_op jit(solution)/shard_map/edges/pallas_call | solution.py:542
  22.8 3.8 %collective-permute-start.3 = (f32[3,32,128]{2,1,0:T(8,128)S(1)}, f32[3,32,128]{2,1,0:T(8,128)S(1)}, u32[]{:S(2)}, u32[]{:S(2)}) collective-permute-start(f32[3,32,128]{2,1,0:T(8,128)S(1)} %get-tuple-element.39), channel_id=1, source_target_pairs={{0,7},{1,0},{2,1},{3,2},{4,3},{5,4},{6,5},{7,6},{8,15},{9,8},{10,9... | collective-permute-start | bytes 147464 | tf_op jit(solution)/shard_map/ppermute | solution.py:36
  26.6 0.0 collective-permute-start.4
  26.6 4.7 %resident.4 = (f32[512,128]{1,0:T(8,128)S(1)}, f32[3,64,128]{2,1,0:T(8,128)S(1)}) custom-call(s32[2,64]{1,0:T(2,128)S(1)} %bitcast.21, s32[1,1]{1,0:T(1,128)S(6)} %copy.18.tally, f32[3,64,128]{2,1,0:T(8,128)S(1)} %get-tuple-element.32.x_ref.rest_0_, f32[3,64,128]{2,1,0:T(8,128)S(1)} %copy-done.1, f32[3,64,128]{2,1,0:T(8,128)S(1)} %bitcast.15, ...), custom_call_target="tpu_custom_call" | custom-call | flops 2000000000 | bytes 1000000 | tf_op jit(solution)/shard_map/resident/pallas_call | solution.py:537
  31.4 0.0 copy-start.8
  31.4 0.3 collective-permute-done.4.lower_x
  31.7 3.0 %edges.4 = (f32[3,64,128]{2,1,0:T(8,128)S(1)}, f32[3,64,128]{2,1,0:T(8,128)S(1)}, f32[3,32,128]{2,1,0:T(8,128)S(1)}, f32[3,32,128]{2,1,0:T(8,128)S(1)}) custom-call(s32[1,32]{1,0:T(1,128)S(1)} %copy-done.5, s32[1,32]{1,0:T(1,128)S(1)} %copy-done.6, s32[2,32]{1,0:T(2,128)S(1)} %bitcast.18, s32[1,1]{1,0:T(1,128)S(6)} %copy.19.tally, ...), custom_call_target="tpu_custom_call" | custom-call | flops 1000000000 | bytes 1000000 | tf_op jit(solution)/shard_map/edges/pallas_call | solution.py:542
  34.7 3.4 %collective-permute-start.5 = (f32[3,32,128]{2,1,0:T(8,128)S(1)}, f32[3,32,128]{2,1,0:T(8,128)S(1)}, u32[]{:S(2)}, u32[]{:S(2)}) collective-permute-start(f32[3,32,128]{2,1,0:T(8,128)S(1)} %get-tuple-element.46), channel_id=1, source_target_pairs={{0,7},{1,0},{2,1},{3,2},{4,3},{5,4},{6,5},{7,6},{8,15},{9,8},{10,9... | collective-permute-start | bytes 147464 | tf_op jit(solution)/shard_map/ppermute | solution.py:36
  38.1 0.0 collective-permute-start.6
  38.1 4.7 %resident.5 = (f32[512,128]{1,0:T(8,128)S(1)}, f32[3,64,128]{2,1,0:T(8,128)S(1)}) custom-call(s32[2,64]{1,0:T(2,128)S(1)} %bitcast.22, s32[1,1]{1,0:T(1,128)S(6)} %copy.18.tally, f32[3,64,128]{2,1,0:T(8,128)S(1)} %get-tuple-element.42.x_ref, f32[3,64,128]{2,1,0:T(8,128)S(1)} %copy-done.1, f32[3,64,128]{2,1,0:T(8,128)S(1)} %get-tuple-element.32.x_ref.rest_0_, ...), custom_call_target="tpu_custom_call" | custom-call | flops 2000000000 | bytes 1000000 | tf_op jit(solution)/shard_map/resident/pallas_call | solution.py:537
  42.8 0.0 collective-permute-done.5.upper_x
  42.8 0.3 collective-permute-done.6.lower_x
  43.1 2.9 %edges.5 = f32[6,64,128]{2,1,0:T(8,128)S(1)} custom-call(s32[1,32]{1,0:T(1,128)S(1)} %copy-done.5, s32[1,32]{1,0:T(1,128)S(1)} %copy-done.6, s32[2,32]{1,0:T(2,128)S(1)} %bitcast.19, s32[1,1]{1,0:T(1,128)S(6)} %copy.19.tally, s32[8,128]{1,0:T(8,128)S(1)} %collective-permute-done.lower, f32[3,64,128]{2,1,0:T(8,128)S(1)} %get-tuple-element.42.x_ref, ...), custom_call_target="tpu_custom_call" | custom-call | flops 1000000000 | bytes 1000000 | tf_op jit(solution)/shard_map/edges/pallas_call | solution.py:542
  46.0 8.0 %collective-permute-start.8 = (f32[6,64,128]{2,1,0:T(8,128)S(1)}, f32[6,64,128]{2,1,0:T(8,128)S(1)}, u32[]{:S(2)}, u32[]{:S(2)}) collective-permute-start(f32[6,64,128]{2,1,0:T(8,128)S(1)} %edges.5), channel_id=1, source_target_pairs={{8,16},{16,8},{24,32},{32,24},{40,48},{48,40},{56,64},{64,56},{72,... | collective-permute-start | bytes 589832 | tf_op jit(solution)/shard_map/ppermute | solution.py:44
  54.0 0.1 collective-permute-start.7
  54.1 0.7 %slice_bitcast_fusion = f32[128]{0:T(128)S(1)} fusion(f32[8,128]{1,0:T(8,128)} %get-tuple-element.25), kind=kLoop, calls=%fused_computation.4 | loop fusion | bytes 1024 | tf_op jit(solution)/shard_map/mul | solution.py:575
  54.8 4.7 %collective-permute-done.8 = f32[6,64,128]{2,1,0:T(8,128)S(1)} collective-permute-done((f32[6,64,128]{2,1,0:T(8,128)S(1)}, f32[6,64,128]{2,1,0:T(8,128)S(1)}, u32[]{:S(2)}, u32[]{:S(2)}) %collective-permute-start.8) | collective-permute-done | bytes 196640 | tf_op jit(solution)/shard_map/ppermute | solution.py:44
  59.5 0.7 %slice_multiply_fusion = (f32[3,64,128]{2,1,0:T(8,128)}, f32[3,64,128]{2,1,0:T(8,128)}) fusion(f32[6,64,128]{2,1,0:T(8,128)S(1)} %select_select_fusion, f32[128]{0:T(128)S(1)} %slice_bitcast_fusion), kind=kLoop, calls=%fused_computation.1 | loop fusion | flops 24576 | bytes 393728 | tf_op jit(solution)/shard_map/mul | solution.py:575
  (19 shorter events, 0.1 us)
Async XLA Ops:
  0.6 18.1 %copy-start.6 = (s32[1,32]{1,0:T(1,128)S(1)}, s32[1,32]{1,0:T(1,128)}, u32[]{:S(2)}) copy-start(s32[1,32]{1,0:T(1,128)} %bottoms.7) | copy-start | bytes 388
  0.6 18.1 %copy-start.5 = (s32[1,32]{1,0:T(1,128)S(1)}, s32[1,32]{1,0:T(1,128)}, u32[]{:S(2)}) copy-start(s32[1,32]{1,0:T(1,128)} %tops.7) | copy-start | bytes 388
  0.7 18.1 %copy-start.4 = (s32[2,1,32]{2,1,0:T(1,128)S(1)}, s32[2,1,32]{2,1,0:T(1,128)}, u32[]{:S(2)}) copy-start(s32[2,1,32]{2,1,0:T(1,128)} %param.19) | copy-start | bytes 772
  0.7 18.1 %copy-start.3 = (f32[3,1,8192]{2,1,0:T(1,128)S(1)}, f32[3,1,8192]{2,1,0:T(1,128)}, u32[]{:S(2)}) copy-start(f32[3,1,8192]{2,1,0:T(1,128)} %param.12) | copy-start | bytes 294916
  0.7 18.1 %copy-start.9 = (f32[3,1,8192]{2,1,0:T(1,128)S(1)}, f32[3,1,8192]{2,1,0:T(1,128)}, u32[]{:S(2)}) copy-start(f32[3,1,8192]{2,1,0:T(1,128)} %param.13) | copy-start | bytes 294916
  3.2 15.4 %collective-permute-start = (s32[8,128]{1,0:T(8,128)}, s32[8,128]{1,0:T(8,128)S(1)}, u32[]{:S(2)}, u32[]{:S(2)}) collective-permute-start(s32[8,128]{1,0:T(8,128)} %get-tuple-element.26), channel_id=1, source_target_pairs={{0,1},{1,2},{2,3},{3,4},{4,5},{5,6},{6,7},{7,0},{8,9},{9,10},{10,1... | collective-permute-start | bytes 12296 | tf_op jit(solution)/shard_map/ppermute | solution.py:36
  5.3 13.4 %collective-permute-start.1 = (f32[5,32,128]{2,1,0:T(8,128)}, f32[5,32,128]{2,1,0:T(8,128)S(1)}, u32[]{:S(2)}, u32[]{:S(2)}) collective-permute-start(f32[5,32,128]{2,1,0:T(8,128)} %get-tuple-element.30), channel_id=1, source_target_pairs={{0,7},{1,0},{2,1},{3,2},{4,3},{5,4},{6,5},{7,6},{8,15},{9,8},{10,9... | collective-permute-start | bytes 245768 | tf_op jit(solution)/shard_map/ppermute | solution.py:36
  8.0 10.7 %collective-permute-start.2 = (f32[5,32,128]{2,1,0:T(8,128)}, f32[5,32,128]{2,1,0:T(8,128)S(1)}, u32[]{:S(2)}, u32[]{:S(2)}) collective-permute-start(f32[5,32,128]{2,1,0:T(8,128)} %get-tuple-element.31), channel_id=1, source_target_pairs={{0,1},{1,2},{2,3},{3,4},{4,5},{5,6},{6,7},{7,0},{8,9},{9,10},{10,1... | collective-permute-start | bytes 245768 | tf_op jit(solution)/shard_map/ppermute | solution.py:36
  9.4 0.9 %copy-start = (f32[3,64,128]{2,1,0:T(8,128)S(1)}, f32[3,64,128]{2,1,0:T(8,128)}, u32[]{:S(2)}) copy-start(f32[3,64,128]{2,1,0:T(8,128)} %get-tuple-element.27.props) | copy-start | bytes 294916
  10.3 0.9 %copy-start.2 = (f32[3,1,8192]{2,1,0:T(1,128)S(1)}, f32[3,1,8192]{2,1,0:T(1,128)}, u32[]{:S(2)}) copy-start(f32[3,1,8192]{2,1,0:T(1,128)} %param.12) | copy-start | bytes 294916
  11.2 0.7 %copy-start.7 = (s32[2,1,64]{2,1,0:T(1,128)S(1)}, s32[2,1,64]{2,1,0:T(1,128)}, u32[]{:S(2)}) copy-start(s32[2,1,64]{2,1,0:T(1,128)} %param.15) | copy-start | bytes 1540
  11.9 0.8 %copy-start.10 = (s32[2,4096]{1,0:T(2,128)S(1)}, s32[2,4096]{1,0:T(2,128)}, u32[]{:S(2)}) copy-start(s32[2,4096]{1,0:T(2,128)} %rest_0_.1) | copy-start | bytes 98308
  12.6 6.1 %copy-start.1 = (f32[3,64,128]{2,1,0:T(8,128)S(1)}, f32[3,64,128]{2,1,0:T(8,128)}, u32[]{:S(2)}) copy-start(f32[3,64,128]{2,1,0:T(8,128)} %get-tuple-element.27.props) | copy-start | bytes 294916
  22.8 8.6 %collective-permute-start.3 = (f32[3,32,128]{2,1,0:T(8,128)S(1)}, f32[3,32,128]{2,1,0:T(8,128)S(1)}, u32[]{:S(2)}, u32[]{:S(2)}) collective-permute-start(f32[3,32,128]{2,1,0:T(8,128)S(1)} %get-tuple-element.39), channel_id=1, source_target_pairs={{0,7},{1,0},{2,1},{3,2},{4,3},{5,4},{6,5},{7,6},{8,15},{9,8},{10,9... | collective-permute-start | bytes 147464 | tf_op jit(solution)/shard_map/ppermute | solution.py:36
  26.6 5.0 %collective-permute-start.4 = (f32[3,32,128]{2,1,0:T(8,128)S(1)}, f32[3,32,128]{2,1,0:T(8,128)S(1)}, u32[]{:S(2)}, u32[]{:S(2)}) collective-permute-start(f32[3,32,128]{2,1,0:T(8,128)S(1)} %get-tuple-element.40), channel_id=1, source_target_pairs={{0,1},{1,2},{2,3},{3,4},{4,5},{5,6},{6,7},{7,0},{8,9},{9,10},{10,1... | collective-permute-start | bytes 147464 | tf_op jit(solution)/shard_map/ppermute | solution.py:36
  31.4 6.7 %copy-start.8 = (s32[2,1,64]{2,1,0:T(1,128)S(1)}, s32[2,1,64]{2,1,0:T(1,128)}, u32[]{:S(2)}) copy-start(s32[2,1,64]{2,1,0:T(1,128)} %param.15) | copy-start | bytes 1540
  34.7 8.1 %collective-permute-start.5 = (f32[3,32,128]{2,1,0:T(8,128)S(1)}, f32[3,32,128]{2,1,0:T(8,128)S(1)}, u32[]{:S(2)}, u32[]{:S(2)}) collective-permute-start(f32[3,32,128]{2,1,0:T(8,128)S(1)} %get-tuple-element.46), channel_id=1, source_target_pairs={{0,7},{1,0},{2,1},{3,2},{4,3},{5,4},{6,5},{7,6},{8,15},{9,8},{10,9... | collective-permute-start | bytes 147464 | tf_op jit(solution)/shard_map/ppermute | solution.py:36
  38.1 5.1 %collective-permute-start.6 = (f32[3,32,128]{2,1,0:T(8,128)S(1)}, f32[3,32,128]{2,1,0:T(8,128)S(1)}, u32[]{:S(2)}, u32[]{:S(2)}) collective-permute-start(f32[3,32,128]{2,1,0:T(8,128)S(1)} %get-tuple-element.47), channel_id=1, source_target_pairs={{0,1},{1,2},{2,3},{3,4},{4,5},{5,6},{6,7},{7,0},{8,9},{9,10},{10,1... | collective-permute-start | bytes 147464 | tf_op jit(solution)/shard_map/ppermute | solution.py:36
  46.0 13.4 %collective-permute-start.8 = (f32[6,64,128]{2,1,0:T(8,128)S(1)}, f32[6,64,128]{2,1,0:T(8,128)S(1)}, u32[]{:S(2)}, u32[]{:S(2)}) collective-permute-start(f32[6,64,128]{2,1,0:T(8,128)S(1)} %edges.5), channel_id=1, source_target_pairs={{8,16},{16,8},{24,32},{32,24},{40,48},{48,40},{56,64},{64,56},{72,... | collective-permute-start | bytes 589832 | tf_op jit(solution)/shard_map/ppermute | solution.py:44
  54.0 5.4 %collective-permute-start.7 = (f32[6,64,128]{2,1,0:T(8,128)S(1)}, f32[6,64,128]{2,1,0:T(8,128)S(1)}, u32[]{:S(2)}, u32[]{:S(2)}) collective-permute-start(f32[6,64,128]{2,1,0:T(8,128)S(1)} %edges.5), channel_id=1, source_target_pairs={{0,8},{8,0},{16,24},{24,16},{32,40},{40,32},{48,56},{56,48},{64,72... | collective-permute-start | bytes 589832 | tf_op jit(solution)/shard_map/ppermute | solution.py:44

commit v2 on v1

--- a/solution.py
+++ b/solution.py
@@ -26,22 +26,31 @@
 BOND_SPREAD = 4
 VMEM_LIMIT = 20 << 20
 PACK_LIMIT = 60 << 20
+PACK_FLOPS = 2000
 
 SMEM = pl.BlockSpec(memory_space=pltpu.SMEM)
 VMEM = pl.BlockSpec(memory_space=pltpu.VMEM)
 
 
-def shifted(shard, axis, by):
-    devices = lax.axis_size(axis)
-    return lax.ppermute(shard, axis, [(i, (i + by) % devices) for i in range(devices)])
-
-
-def swapped(shard, axis, start):
+def swapped(shard, axis, start, ring=False):
     devices = lax.axis_size(axis)
     pairs = []
-    for i in range(start, devices - 1, 2):
-        pairs += [(i, i + 1), (i + 1, i)]
+    for i in range(start, devices if ring else devices - 1, 2):
+        other = (i + 1) % devices
+        pairs += [(i, other), (other, i)]
     return lax.ppermute(shard, axis, pairs)
+
+
+def side_lists(tops, bottoms):
+    odd = lax.rem(lax.axis_index("dom"), 2) == 1
+
+    def first(k):
+        return jnp.where(odd, bottoms[0, k], tops[0, k])
+
+    def second(k):
+        return jnp.where(odd, tops[0, k], bottoms[0, k])
+
+    return odd, first, second
 
 
 def halves(a):
@@ -221,7 +230,9 @@
 
 def local_kernel(first, pairs, tally, x_ref, props, *rest):
     if first:
-        bonds, acc, bonded, picks, masks, ratio, *scratch = rest
+        raw = props
+        bonds, acc, bonded, props, picks, masks, ratio, *scratch = rest
+        relay_properties(raw, props)
     else:
         x_before, bonded_before, picks, masks, ratio, acc, bonded, *scratch = rest
     stacks, moment_rows, near, far, moments, rho, table, bond_sums = scratch
@@ -298,39 +309,29 @@
             bonded[c, pl.ds(k * half, half), :] = new
 
 
-def edge_kernel(
-    first,
-    last,
-    kick,
-    tops,
-    bottoms,
-    slots,
-    tally,
-    lower,
-    x_ref,
-    v_ref,
-    props,
-    acc_in,
-    bonded,
-    upper_x,
-    lower_x,
-    upper_start,
-    lower_start,
-    *rest,
-):
-    *rest, stacks, moment_rows, near, far, moments, rho, acc = rest
+def edge_kernel(first, last, kick, tops, bottoms, slots, tally, *rest):
     if last:
-        ratio, state = rest
+        levels, mates, *rest = rest
+    x_ref, v_ref, props, acc_in, bonded, first_x, second_x, first_start, second_start, *rest = rest
+    *rest, stacks, moment_rows, near, far, moments, rho, acc, indices, lower, arrived = rest
+    if last:
+        ratio, state, choice = rest
+        exchange_choice(levels, mates, choice)
     elif first:
-        x_out, v_out, to_upper, to_lower, ratio = rest
+        x_out, v_out, to_first, to_second, ratio = rest
     else:
-        ratio, x_out, v_out, to_upper, to_lower = rest
+        ratio, x_out, v_out, to_first, to_second = rest
+    odd, _, _ = side_lists(tops, bottoms)
+    rows = [start[5, pl.ds(0, ROWS), :] for start in (first_start, second_start)]
+    indices[...] = jnp.where(odd, rows[0], rows[1]).astype(jnp.int32)
+    fetch = pltpu.make_async_copy(indices, lower, arrived)
+    fetch.start()
     clusters = x_ref.shape[1]
-    facing = upper_x.shape[1]
+    facing = first_x.shape[1]
     parts = position_parts(x_ref[0], x_ref[1], x_ref[2])
     far_stack(stacks, *parts)
     rho[...] = charge_ratio(props[0], props[1])
-    for side, (hx, hp) in enumerate(((upper_x, upper_start), (lower_x, lower_start))):
+    for side, (hx, hp) in enumerate(((first_x, first_start), (second_x, second_start))):
         if first:
             fill_ratio(ratio, charge_ratio(hp[3], hp[4]), side * facing)
         near_stack(stacks, side * facing, *position_parts(hx[0], hx[1], hx[2]))
@@ -343,11 +344,14 @@
     acc[...] = acc_in[...]
 
     width = slots.shape[1]
+    upper_base = jnp.where(odd, facing, 0)
+    lower_base = facing - upper_base
+    fetch.wait()
     ends, weights = [], []
     for s in range(width):
-        ends.append((slots[1, s], tops[0, slots[0, s]]))
+        ends.append((upper_base + slots[1, s], tops[0, slots[0, s]]))
         weights.append(jnp.where(s < tally[0, 0], 1.0, 0.0))
-        ends.append((facing + lower[0, s], bottoms[0, lower[1, s]]))
+        ends.append((lower_base + lower[0, s], bottoms[0, lower[1, s]]))
         weights.append(jnp.where(s < lower[2, 0], 1.0, 0.0))
     count = len(ends)
     products, scales = [None] * count, [None] * count
@@ -381,31 +385,37 @@
             v_out[c] = v
             x_out[c] = x_ref[c] + TIME_STEP * v
     if not last:
-        pack_rows(tops, bottoms, x_out, to_upper, to_lower, 0, 3)
-
-
-def pack_rows(tops, bottoms, source, to_upper, to_lower, base, count):
-    for k in range(to_upper.shape[1]):
-        i, j = tops[0, k], bottoms[0, k]
-        up = [source[c, pl.ds(i, 1), :] for c in range(count)]
-        down = [source[c, pl.ds(j, 1), :] for c in range(count)]
+        pack_rows(tops, bottoms, x_out, to_first, to_second, 0, 3)
+
+
+def pack_rows(tops, bottoms, source, to_first, to_second, base, count):
+    _, first, second = side_lists(tops, bottoms)
+    for k in range(to_first.shape[1]):
+        i, j = first(k), second(k)
+        rows = [[source[c, pl.ds(n, 1), :] for c in range(count)] for n in (i, j)]
         for c in range(count):
-            to_upper[base + c, pl.ds(k, 1), :] = up[c]
-            to_lower[base + c, pl.ds(k, 1), :] = down[c]
-
-
-def pack_kernel(
-    tops, bottoms, levels, mates, x_ref, raw, slots, tally, props, to_upper, to_lower, index_rows, choice
-):
-    for c in range(3):
+            to_first[base + c, pl.ds(k, 1), :] = rows[0][c]
+            to_second[base + c, pl.ds(k, 1), :] = rows[1][c]
+
+
+def relay_properties(raw, props):
+    for c in range(props.shape[0]):
         for k in range(props.shape[1]):
             props[c, pl.ds(k, 1), :] = raw[pl.ds(c, 1), pl.ds(k * CA, CA)]
-    pack_rows(tops, bottoms, x_ref, to_upper, to_lower, 0, 3)
-    pack_rows(tops, bottoms, props, to_upper, to_lower, 3, 2)
+
+
+def pack_kernel(tops, bottoms, x_ref, raw, slots, tally, to_first, to_second, props):
+    relay_properties(raw, props)
     width = slots.shape[1]
-    index_rows[...] = jnp.zeros_like(index_rows)
-    index_rows[pl.ds(0, 2), pl.ds(0, width)] = slots[...]
-    index_rows[pl.ds(2, 1), pl.ds(0, 1)] = tally[...]
+    for buffer in (to_first, to_second):
+        buffer[5] = jnp.zeros(buffer.shape[1:], F32)
+        buffer[5, pl.ds(0, 2), pl.ds(0, width)] = slots[...].astype(F32)
+        buffer[5, pl.ds(2, 1), pl.ds(0, 1)] = tally[...].astype(F32)
+    pack_rows(tops, bottoms, x_ref, to_first, to_second, 0, 3)
+    pack_rows(tops, bottoms, props, to_first, to_second, 3, 2)
+
+
+def exchange_choice(levels, mates, choice):
     own = lax.axis_index("rep")
     mate = mates[own]
     near_mate = own + 1 - 2 * lax.rem(own, 2)
@@ -442,32 +452,27 @@
     sds = jax.ShapeDtypeStruct
     params = pltpu.CompilerParams(vmem_limit_bytes=VMEM_LIMIT)
 
-    props, to_upper, to_lower, index_rows, choice = pl.pallas_call(
+    to_first, to_second = pl.pallas_call(
         pack_kernel,
-        out_shape=(
-            sds(shape, F32),
-            sds((5, facing, CA), F32),
-            sds((5, facing, CA), F32),
-            sds((ROWS, CA), jnp.int32),
-            sds((ROWS, CA), F32),
+        out_shape=(sds((6, facing, CA), F32),) * 2,
+        in_specs=[SMEM] * 2 + [VMEM] * 4,
+        out_specs=(VMEM,) * 2,
+        scratch_shapes=[pltpu.VMEM((2,) + shape[1:], F32)],
+        compiler_params=pltpu.CompilerParams(vmem_limit_bytes=PACK_LIMIT),
+        cost_estimate=pl.CostEstimate(
+            flops=PACK_FLOPS * 1_000_000, bytes_accessed=1_000_000, transcendentals=0
         ),
-        in_specs=[SMEM] * 4 + [VMEM] * 4,
-        out_specs=(VMEM,) * 5,
-        compiler_params=pltpu.CompilerParams(vmem_limit_bytes=PACK_LIMIT),
         name="pack",
     )(
         top_edge_groups,
         bottom_edge_groups,
-        thermal_levels,
-        exchange_mate,
         x,
         atomic_properties,
         slots,
         boundary_tile_tally,
     )
-    upper_start = shifted(to_lower, "dom", -1)
-    lower_start = shifted(to_upper, "dom", 1)
-    lower = shifted(index_rows, "dom", 1)
+    first_start = swapped(to_first, "dom", 0, True)
+    second_start = swapped(to_second, "dom", 1, True)
 
     def scratch(sources):
         return [
@@ -481,6 +486,7 @@
 
     bonds = spring_links.shape[1]
     kept = (
+        sds(shape, F32),
         sds((2, 2 * CA, bonds), BF16),
         sds((2, clusters // 2, bonds), BF16),
         sds((clusters, CA, CA), F32),
@@ -493,7 +499,7 @@
             functools.partial(local_kernel, first),
             out_shape=sums + kept if first else sums,
             in_specs=[SMEM] * 2 + [VMEM] * (3 if first else 7),
-            out_specs=(VMEM,) * (5 if first else 2),
+            out_specs=(VMEM,) * (6 if first else 2),
             scratch_shapes=scratch(clusters)
             + [
                 pltpu.VMEM((rows, 2 * CA), BF16),
@@ -508,7 +514,7 @@
 
     def edge_call(first, last, kick):
         if last:
-            outs = (sds((6, clusters, CA), F32),)
+            outs = (sds((6, clusters, CA), F32), sds((ROWS, CA), F32))
         else:
             outs = (sds(shape, F32),) * 2 + (sds((3, facing, CA), F32),) * 2
         if first:
@@ -516,9 +522,15 @@
         return pl.pallas_call(
             functools.partial(edge_kernel, first, last, kick),
             out_shape=outs,
-            in_specs=[SMEM] * 5 + [VMEM] * (9 if first else 10),
+            in_specs=[SMEM] * (6 if last else 4) + [VMEM] * (9 if first else 10),
             out_specs=(VMEM,) * len(outs),
-            scratch_shapes=scratch(2 * facing) + [pltpu.VMEM((clusters * ROWS, CA), F32)],
+            scratch_shapes=scratch(2 * facing)
+            + [
+                pltpu.VMEM((clusters * ROWS, CA), F32),
+                pltpu.VMEM((ROWS, CA), jnp.int32),
+                pltpu.SMEM((ROWS, CA), jnp.int32),
+                pltpu.SemaphoreType.DMA,
+            ],
             compiler_params=params,
             cost_estimate=pl.CostEstimate(
                 flops=1_000_000_000, bytes_accessed=1_000_000, transcendentals=2_000_000
@@ -527,11 +539,11 @@
         )
 
     halo_ratio = ()
-    upper_x, lower_x = upper_start, lower_start
+    first_x, second_x = first_start, second_start
     for step in range(STEPS + 1):
         if step == 0:
-            acc, bonded, *static = local_call(True)(
-                pairs, resident_tile_tally, x, props, spring_links
+            acc, bonded, props, *static = local_call(True)(
+                pairs, resident_tile_tally, x, atomic_properties, spring_links
             )
         else:
             acc, bonded = local_call(False)(
@@ -544,26 +556,26 @@
             bottom_edge_groups,
             slots,
             boundary_tile_tally,
-            lower,
+            *((thermal_levels, exchange_mate) if last else ()),
             x,
             v,
             props,
             acc,
             bonded,
-            upper_x,
-            lower_x,
-            upper_start,
-            lower_start,
+            first_x,
+            second_x,
+            first_start,
+            second_start,
             *halo_ratio,
         )
         if last:
-            (state,) = results
+            state, choice = results
         else:
             x_before = x
-            x, v, to_upper, to_lower, *new_ratio = results
+            x, v, to_first, to_second, *new_ratio = results
             halo_ratio = halo_ratio or new_ratio
-            upper_x = shifted(to_lower, "dom", -1)
-            lower_x = shifted(to_upper, "dom", 1)
+            first_x = swapped(to_first, "dom", 0, True)
+            second_x = swapped(to_second, "dom", 1, True)
 
     keep, near_mate, ratio = choice[0] > 0.5, choice[1] > 0.5, choice[2]
 

time: 60.9 us -> 53.3 us (0.88)
  local copies, waits for them, and re-layouts: 3.94 us -> 0.05 us
  starting transfers between devices: 20 us -> 16.3 us
  Pallas kernels: 27.3 us -> 28.5 us
  other arithmetic: 1.5 us -> 0.74 us
    ppermute x7 -> x0, starting transfers between devices: 11.9 us -> none  [shifted(): lax.ppermute(shard, axis, [(i, (i + by) % devices) for i in range(devices)])]
    ppermute x2 -> x8, starting transfers between devices: 8.09 us -> 16.3 us  [swapped(): return lax.ppermute(shard, axis, pairs)]
    unnamed x22 -> x20, local copies, waits for them, and re-layouts: 3.25 us -> 0.04 us
    pallas_call x3, Pallas kernels: 9.96 us -> 11.1 us  [local(): edge_call(step == 0, last, kick)]
    gt x1, other arithmetic: 0.77 us -> 0.01 us  [local(): keep, near_mate, ratio = (choice[0] > 0.5, choice[1] > 0.5, choice[2])]
    mul x1, local copies, waits for them, and re-layouts: 0.69 us -> 0.01 us  [local(): return (new[:3].reshape(out), (new[3:] * ratio).reshape(out))]
    ppermute x2 -> x8, waiting for transfers between devices: 4.66 us -> 5.34 us  [swapped(): return lax.ppermute(shard, axis, pairs)]
    ppermute x7 -> x0, waiting for transfers between devices: 0.65 us -> none  [shifted(): lax.ppermute(shard, axis, [(i, (i + by) % devices) for i in range(devices)])]
  transfers between devices with their start and end apart: 9 -> 8, of which waited for: 3 -> 1; matrix products, arithmetic and copies ran while one was open for 2% -> 0% of each run, Pallas kernels for 26% -> 29%
where the time goes in v2:
time: 53.3 us; the launch traced here: 53.1 us
  Pallas kernels  28.5 us (53%)
  starting transfers between devices  16.3 us (31%)
  waiting for transfers between devices  5.34 us (10%)
  between operations  2.22 us (4%)
  other arithmetic  0.74 us (1%)
    ppermute x8, starting transfers between devices, swapped(): return lax.ppermute(shard, axis, pairs)  16.3 us
    pallas_call x3, Pallas kernels, local(): edge_call(step == 0, last, kick)  11.1 us
    pallas_call x2, Pallas kernels, local(): local_call(False)  9.44 us
    pallas_call x1, Pallas kernels, local(): local_call(True)  6.11 us
    ppermute x8, waiting for transfers between devices, swapped(): return lax.ppermute(shard, axis, pairs)  5.34 us
    pallas_call x1, Pallas kernels, local(): pl.pallas_call(pack_kernel, out_shape=(sds((6, facing, CA), F32),) * 2, i...  1.87 us
  transfers between devices with their start and end apart: 8, of which 1 were waited for; matrix products, arithmetic and copies ran while one was open for 0% of the time, Pallas kernels for 29%

profile of v2, /device:TPU:1, one launch (start us, length us, event | category | flops | bytes accessed | tf_op | source)
XLA Modules:
  0.0 53.1 jit_solution(1548565193004415316)
XLA Ops:
  0.6 0.0 copy-start.7
  0.6 0.0 copy-start
  0.7 0.0 copy-start.9
  0.7 0.0 copy-start.1
  1.4 1.9 %pack.1 = (f32[6,32,128]{2,1,0:T(8,128)}, f32[6,32,128]{2,1,0:T(8,128)}) custom-call(s32[1,32]{1,0:T(1,128)} %tops.7, s32[1,32]{1,0:T(1,128)} %bottoms.7, f32[3,64,128]{2,1,0:T(8,128)} %bitcast.12, f32[3,8192]{1,0:T(4,128)} %raw.1, s32[2,32]{1,0:T(2,128)} %bitcast.19, s32[1,1]{1,0:T(1,128)S(6)} %copy.19.tally), custom_call_target="tpu_custom_call" | custom-call | flops 2000000000 | bytes 1000000 | tf_op jit(solution)/shard_map/pack/pallas_call | solution.py:455
  3.2 0.0 copy-start.8
  3.3 2.1 %collective-permute-start = (f32[6,32,128]{2,1,0:T(8,128)}, f32[6,32,128]{2,1,0:T(8,128)S(1)}, u32[]{:S(2)}, u32[]{:S(2)}) collective-permute-start(f32[6,32,128]{2,1,0:T(8,128)} %get-tuple-element.28), channel_id=1, source_target_pairs={{0,1},{1,0},{2,3},{3,2},{4,5},{5,4},{6,7},{7,6},{8,9},{9,8},{10,11... | collective-permute-start | bytes 294920 | tf_op jit(solution)/shard_map/ppermute | solution.py:41
  5.4 3.2 %collective-permute-start.1 = (f32[6,32,128]{2,1,0:T(8,128)}, f32[6,32,128]{2,1,0:T(8,128)S(1)}, u32[]{:S(2)}, u32[]{:S(2)}) collective-permute-start(f32[6,32,128]{2,1,0:T(8,128)} %get-tuple-element.29), channel_id=1, source_target_pairs={{1,2},{2,1},{3,4},{4,3},{5,6},{6,5},{7,0},{0,7},{9,10},{10,9},{11,... | collective-permute-start | bytes 294920 | tf_op jit(solution)/shard_map/ppermute | solution.py:41
  9.2 0.0 copy-done.7
  9.2 0.0 copy-done
  9.2 0.0 copy-done.9
  9.2 6.1 %resident.3 = (f32[512,128]{1,0:T(8,128)S(1)}, f32[3,64,128]{2,1,0:T(8,128)S(1)}, f32[3,64,128]{2,1,0:T(8,128)S(1)}, bf16[2,256,4096]{2,1,0:T(8,128)(2,1)S(1)}, ...) custom-call(s32[2,64]{1,0:T(2,128)S(1)} %bitcast.16, s32[1,1]{1,0:T(1,128)S(6)} %copy.18.tally, ...), custom_call_target="tpu_custom_call" | custom-call | flops 2000000000 | bytes 1000000 | tf_op jit(solution)/shard_map/resident/pallas_call | solution.py:545
  15.3 0.0 collective-permute-done.rest_5_.rest_7_.rest_9_
  15.3 0.0 collective-permute-done.1.rest_6_.rest_8_.rest_10_
  15.4 4.4 %edges.3 = (f32[3,64,128]{2,1,0:T(8,128)S(1)}, f32[3,64,128]{2,1,0:T(8,128)S(1)}, f32[3,32,128]{2,1,0:T(8,128)S(1)}, f32[3,32,128]{2,1,0:T(8,128)S(1)}, f32[64,128,128]{2,1,0:T(8,128)S(1)}) custom-call(s32[1,32]{1,0:T(1,128)S(1)} %copy-done.3, s32[1,32]{1,0:T(1,128)S(1)} %copy-done.4, s32[2,32]{1,0:T(2,128)S(1)} %bitcast.20, s32[1,1]{1,0:T(1,128)S(6)} %copy.19.tally, ...), custom_call_target="tpu_custom_call" | custom-call | flops 1000000000 | bytes 1000000 | tf_op jit(solution)/shard_map/edges/pallas_call | solution.py:554
  19.8 0.1 collective-permute-start.2
  19.9 0.9 %collective-permute-start.3 = (f32[3,32,128]{2,1,0:T(8,128)S(1)}, f32[3,32,128]{2,1,0:T(8,128)S(1)}, u32[]{:S(2)}, u32[]{:S(2)}) collective-permute-start(f32[3,32,128]{2,1,0:T(8,128)S(1)} %get-tuple-element.38), channel_id=1, source_target_pairs={{1,2},{2,1},{3,4},{4,3},{5,6},{6,5},{7,0},{0,7},{9,10},{10,9},{11,... | collective-permute-start | bytes 147464 | tf_op jit(solution)/shard_map/ppermute | solution.py:41
  20.8 4.7 %resident.4 = (f32[512,128]{1,0:T(8,128)S(1)}, f32[3,64,128]{2,1,0:T(8,128)S(1)}) custom-call(s32[2,64]{1,0:T(2,128)S(1)} %bitcast.17, s32[1,1]{1,0:T(1,128)S(6)} %copy.18.tally, f32[3,64,128]{2,1,0:T(8,128)S(1)} %get-tuple-element.30.x_ref.rest_0_, f32[3,64,128]{2,1,0:T(8,128)S(1)} %get-tuple-element.25.rest_2_.props.rest_4_, f32[3,64,128]{2,1,0:T(8,128)S(1)} %bitcast.15, ...), custom_call_target="tpu_custom_call" | custom-call | flops 2000000000 | bytes 1000000 | tf_op jit(solution)/shard_map/resident/pallas_call | solution.py:549
  25.5 0.0 collective-permute-done.2.rest_5_
  25.5 0.0 collective-permute-done.3.rest_6_
  25.5 3.4 %edges.4 = (f32[3,64,128]{2,1,0:T(8,128)S(1)}, f32[3,64,128]{2,1,0:T(8,128)S(1)}, f32[3,32,128]{2,1,0:T(8,128)S(1)}, f32[3,32,128]{2,1,0:T(8,128)S(1)}) custom-call(s32[1,32]{1,0:T(1,128)S(1)} %copy-done.3, s32[1,32]{1,0:T(1,128)S(1)} %copy-done.4, s32[2,32]{1,0:T(2,128)S(1)} %bitcast.21, s32[1,1]{1,0:T(1,128)S(6)} %copy.19.tally, ...), custom_call_target="tpu_custom_call" | custom-call | flops 1000000000 | bytes 1000000 | tf_op jit(solution)/shard_map/edges/pallas_call | solution.py:554
  28.9 0.9 %collective-permute-start.4 = (f32[3,32,128]{2,1,0:T(8,128)S(1)}, f32[3,32,128]{2,1,0:T(8,128)S(1)}, u32[]{:S(2)}, u32[]{:S(2)}) collective-permute-start(f32[3,32,128]{2,1,0:T(8,128)S(1)} %get-tuple-element.44), channel_id=1, source_target_pairs={{0,1},{1,0},{2,3},{3,2},{4,5},{5,4},{6,7},{7,6},{8,9},{9,8},{10,11... | collective-permute-start | bytes 147464 | tf_op jit(solution)/shard_map/ppermute | solution.py:41
  29.8 2.5 %collective-permute-start.5 = (f32[3,32,128]{2,1,0:T(8,128)S(1)}, f32[3,32,128]{2,1,0:T(8,128)S(1)}, u32[]{:S(2)}, u32[]{:S(2)}) collective-permute-start(f32[3,32,128]{2,1,0:T(8,128)S(1)} %get-tuple-element.45), channel_id=1, source_target_pairs={{1,2},{2,1},{3,4},{4,3},{5,6},{6,5},{7,0},{0,7},{9,10},{10,9},{11,... | collective-permute-start | bytes 147464 | tf_op jit(solution)/shard_map/ppermute | solution.py:41
  32.3 4.7 %resident.5 = (f32[512,128]{1,0:T(8,128)S(1)}, f32[3,64,128]{2,1,0:T(8,128)S(1)}) custom-call(s32[2,64]{1,0:T(2,128)S(1)} %bitcast.18, s32[1,1]{1,0:T(1,128)S(6)} %copy.18.tally, f32[3,64,128]{2,1,0:T(8,128)S(1)} %get-tuple-element.40.x_ref.rest_2_, f32[3,64,128]{2,1,0:T(8,128)S(1)} %get-tuple-element.25.rest_2_.props.rest_4_, ...), custom_call_target="tpu_custom_call" | custom-call | flops 2000000000 | bytes 1000000 | tf_op jit(solution)/shard_map/resident/pallas_call | solution.py:549
  37.0 0.0 collective-permute-done.4.rest_7_
  37.0 0.0 collective-permute-done.5.rest_8_
  37.1 3.3 %edges.5 = (f32[6,64,128]{2,1,0:T(8,128)S(1)}, f32[8,128]{1,0:T(8,128)S(1)}) custom-call(s32[1,32]{1,0:T(1,128)S(1)} %copy-done.3, s32[1,32]{1,0:T(1,128)S(1)} %copy-done.4, s32[2,32]{1,0:T(2,128)S(1)} %bitcast.22, s32[1,1]{1,0:T(1,128)S(6)} %copy.19.tally, f32[32]{0:T(128)S(1)} %copy-done.5, s32[32]{0:T(128)S(1)} %copy-done.6, ...), custom_call_target="tpu_custom_call" | custom-call | flops 1000000000 | bytes 1000000 | tf_op jit(solution)/shard_map/edges/pallas_call | solution.py:554
  40.4 6.6 %collective-permute-start.7 = (f32[6,64,128]{2,1,0:T(8,128)S(1)}, f32[6,64,128]{2,1,0:T(8,128)S(1)}, u32[]{:S(2)}, u32[]{:S(2)}) collective-permute-start(f32[6,64,128]{2,1,0:T(8,128)S(1)} %get-tuple-element.47), channel_id=1, source_target_pairs={{8,16},{16,8},{24,32},{32,24},{40,48},{48,40},{56,64},{64,56},{72,... | collective-permute-start | bytes 589832 | tf_op jit(solution)/shard_map/ppermute | solution.py:41
  47.0 0.1 collective-permute-start.6
  47.1 5.3 %collective-permute-done.7 = f32[6,64,128]{2,1,0:T(8,128)S(1)} collective-permute-done((f32[6,64,128]{2,1,0:T(8,128)S(1)}, f32[6,64,128]{2,1,0:T(8,128)S(1)}, u32[]{:S(2)}, u32[]{:S(2)}) %collective-permute-start.7) | collective-permute-done | bytes 196640 | tf_op jit(solution)/shard_map/ppermute | solution.py:41
  52.4 0.0 collective-permute-done.6
  52.4 0.7 %slice_multiply_fusion = (f32[3,64,128]{2,1,0:T(8,128)}, f32[3,64,128]{2,1,0:T(8,128)}) fusion(f32[6,64,128]{2,1,0:T(8,128)S(1)} %select_select_fusion, f32[128]{0:T(128)S(1)} %slice_bitcast_fusion), kind=kLoop, calls=%fused_computation.1 | loop fusion | flops 24576 | bytes 393728 | tf_op jit(solution)/shard_map/mul | solution.py:587
  (15 shorter events, 0.1 us)
Async XLA Ops:
  0.6 8.6 %copy-start.7 = (f32[3,8192]{1,0:T(4,128)S(1)}, f32[3,8192]{1,0:T(4,128)}, u32[]{:S(2)}) copy-start(f32[3,8192]{1,0:T(4,128)} %raw.1) | copy-start | bytes 294916
  0.6 8.6 %copy-start = (f32[3,1,8192]{2,1,0:T(1,128)S(1)}, f32[3,1,8192]{2,1,0:T(1,128)}, u32[]{:S(2)}) copy-start(f32[3,1,8192]{2,1,0:T(1,128)} %param.12) | copy-start | bytes 294916
  0.7 8.6 %copy-start.9 = (s32[2,4096]{1,0:T(2,128)S(1)}, s32[2,4096]{1,0:T(2,128)}, u32[]{:S(2)}) copy-start(s32[2,4096]{1,0:T(2,128)} %rest_0_.2) | copy-start | bytes 98308
  0.7 8.6 %copy-start.1 = (s32[2,1,64]{2,1,0:T(1,128)S(1)}, s32[2,1,64]{2,1,0:T(1,128)}, u32[]{:S(2)}) copy-start(s32[2,1,64]{2,1,0:T(1,128)} %param.15) | copy-start | bytes 1540
  3.2 12.1 %copy-start.2 = (s32[2,1,32]{2,1,0:T(1,128)S(1)}, s32[2,1,32]{2,1,0:T(1,128)}, u32[]{:S(2)}) copy-start(s32[2,1,32]{2,1,0:T(1,128)} %param.19) | copy-start | bytes 772
  3.2 12.1 %copy-start.3 = (s32[1,32]{1,0:T(1,128)S(1)}, s32[1,32]{1,0:T(1,128)}, u32[]{:S(2)}) copy-start(s32[1,32]{1,0:T(1,128)} %tops.7) | copy-start | bytes 388
  3.2 12.1 %copy-start.4 = (s32[1,32]{1,0:T(1,128)S(1)}, s32[1,32]{1,0:T(1,128)}, u32[]{:S(2)}) copy-start(s32[1,32]{1,0:T(1,128)} %bottoms.7) | copy-start | bytes 388
  3.2 12.2 %copy-start.8 = (f32[3,1,8192]{2,1,0:T(1,128)S(1)}, f32[3,1,8192]{2,1,0:T(1,128)}, u32[]{:S(2)}) copy-start(f32[3,1,8192]{2,1,0:T(1,128)} %param.13) | copy-start | bytes 294916
  3.3 12.1 %collective-permute-start = (f32[6,32,128]{2,1,0:T(8,128)}, f32[6,32,128]{2,1,0:T(8,128)S(1)}, u32[]{:S(2)}, u32[]{:S(2)}) collective-permute-start(f32[6,32,128]{2,1,0:T(8,128)} %get-tuple-element.28), channel_id=1, source_target_pairs={{0,1},{1,0},{2,3},{3,2},{4,5},{5,4},{6,7},{7,6},{8,9},{9,8},{10,11... | collective-permute-start | bytes 294920 | tf_op jit(solution)/shard_map/ppermute | solution.py:41
  5.4 10.0 %collective-permute-start.1 = (f32[6,32,128]{2,1,0:T(8,128)}, f32[6,32,128]{2,1,0:T(8,128)S(1)}, u32[]{:S(2)}, u32[]{:S(2)}) collective-permute-start(f32[6,32,128]{2,1,0:T(8,128)} %get-tuple-element.29), channel_id=1, source_target_pairs={{1,2},{2,1},{3,4},{4,3},{5,6},{6,5},{7,0},{0,7},{9,10},{10,9},{11,... | collective-permute-start | bytes 294920 | tf_op jit(solution)/shard_map/ppermute | solution.py:41
  19.8 5.7 %collective-permute-start.2 = (f32[3,32,128]{2,1,0:T(8,128)S(1)}, f32[3,32,128]{2,1,0:T(8,128)S(1)}, u32[]{:S(2)}, u32[]{:S(2)}) collective-permute-start(f32[3,32,128]{2,1,0:T(8,128)S(1)} %get-tuple-element.37), channel_id=1, source_target_pairs={{0,1},{1,0},{2,3},{3,2},{4,5},{5,4},{6,7},{7,6},{8,9},{9,8},{10,11... | collective-permute-start | bytes 147464 | tf_op jit(solution)/shard_map/ppermute | solution.py:41
  19.9 5.6 %collective-permute-start.3 = (f32[3,32,128]{2,1,0:T(8,128)S(1)}, f32[3,32,128]{2,1,0:T(8,128)S(1)}, u32[]{:S(2)}, u32[]{:S(2)}) collective-permute-start(f32[3,32,128]{2,1,0:T(8,128)S(1)} %get-tuple-element.38), channel_id=1, source_target_pairs={{1,2},{2,1},{3,4},{4,3},{5,6},{6,5},{7,0},{0,7},{9,10},{10,9},{11,... | collective-permute-start | bytes 147464 | tf_op jit(solution)/shard_map/ppermute | solution.py:41
  28.9 8.1 %collective-permute-start.4 = (f32[3,32,128]{2,1,0:T(8,128)S(1)}, f32[3,32,128]{2,1,0:T(8,128)S(1)}, u32[]{:S(2)}, u32[]{:S(2)}) collective-permute-start(f32[3,32,128]{2,1,0:T(8,128)S(1)} %get-tuple-element.44), channel_id=1, source_target_pairs={{0,1},{1,0},{2,3},{3,2},{4,5},{5,4},{6,7},{7,6},{8,9},{9,8},{10,11... | collective-permute-start | bytes 147464 | tf_op jit(solution)/shard_map/ppermute | solution.py:41
  29.8 7.2 %collective-permute-start.5 = (f32[3,32,128]{2,1,0:T(8,128)S(1)}, f32[3,32,128]{2,1,0:T(8,128)S(1)}, u32[]{:S(2)}, u32[]{:S(2)}) collective-permute-start(f32[3,32,128]{2,1,0:T(8,128)S(1)} %get-tuple-element.45), channel_id=1, source_target_pairs={{1,2},{2,1},{3,4},{4,3},{5,6},{6,5},{7,0},{0,7},{9,10},{10,9},{11,... | collective-permute-start | bytes 147464 | tf_op jit(solution)/shard_map/ppermute | solution.py:41
  32.3 4.8 %copy-start.5 = (f32[32]{0:T(128)S(1)}, f32[32]{0:T(128)}, u32[]{:S(2)}) copy-start(f32[32]{0:T(128)} %rest_0_.3) | copy-start | bytes 388
  32.3 4.8 %copy-start.6 = (s32[32]{0:T(128)S(1)}, s32[32]{0:T(128)}, u32[]{:S(2)}) copy-start(s32[32]{0:T(128)} %rest_1_.1) | copy-start | bytes 388
  40.4 12.0 %collective-permute-start.7 = (f32[6,64,128]{2,1,0:T(8,128)S(1)}, f32[6,64,128]{2,1,0:T(8,128)S(1)}, u32[]{:S(2)}, u32[]{:S(2)}) collective-permute-start(f32[6,64,128]{2,1,0:T(8,128)S(1)} %get-tuple-element.47), channel_id=1, source_target_pairs={{8,16},{16,8},{24,32},{32,24},{40,48},{48,40},{56,64},{64,56},{72,... | collective-permute-start | bytes 589832 | tf_op jit(solution)/shard_map/ppermute | solution.py:41
  47.0 5.4 %collective-permute-start.6 = (f32[6,64,128]{2,1,0:T(8,128)S(1)}, f32[6,64,128]{2,1,0:T(8,128)S(1)}, u32[]{:S(2)}, u32[]{:S(2)}) collective-permute-start(f32[6,64,128]{2,1,0:T(8,128)S(1)} %get-tuple-element.47), channel_id=1, source_target_pairs={{0,8},{8,0},{16,24},{24,16},{32,40},{40,32},{48,56},{56,48},{64,72... | collective-permute-start | bytes 589832 | tf_op jit(solution)/shard_map/ppermute | solution.py:41
